TPU v7x, 32 devices: a whole 2x2x4 slice. The times are simulated.
32 devices in a mesh: tm: 8 (over z, x), series: 4 (over y, core).
Axes of the slice: x: 2, y: 2, z: 4, core: 2. Of those that a mesh axis runs over, the one named last changes fastest.
Arguments:
- readings: bfloat16 [128, 4096], P('tm', 'series'), may hold values from -8 to 8
- present: int32 [128, 4096], P('tm', 'series'), may hold values 0 or 1
- loadings: bfloat16 [4096, 128], P('series'), may hold values from -1 to 1
- noise_precision: float32 [4096], P('series'), may hold values from 0.5 to 2
- update_gain: float32 [128], replicated, may hold values from 3.125e-05 to 0.03125
- factor_rate: float32 [128], replicated, may hold values from 0.0001 to 0.01
- smooth_rate: float32 [128], replicated, may hold values from 0.0001 to 0.05
- regions: int32 [4096], P('series'), may hold values from 0 to 15
Outputs:
- smoothed: float32 [128, 128], P('tm')
- histogram: float32 [16, 20], replicated
All inputs are finite; a program needn't handle non-finite values. No bound on the sum of `present` on one device may be relied on, other than what follows from the above.
Results may differ from a plain program's by a relative error of at most 0.0004.
Values sent between devices are 32-bit elements; how exact they have to be, the bound alone decides.
A program may use at most 64 MiB of HBM per device.

v0:
```python
import functools

import jax
import jax.numpy as jnp
from jax import lax
from jax.experimental import pallas as pl
from jax.experimental.pallas import tpu as pltpu
from jax.sharding import PartitionSpec as P

BINS = 20
GROUPS = 16
MESH = pl.DeviceIdType.MESH
F32 = jnp.float32
BF16 = jnp.bfloat16


def split2(x):
    high = x.astype(BF16)
    return high, (x - high.astype(F32)).astype(BF16)


def halves(right):
    high, low = split2(right)
    return jnp.concatenate([high, low], axis=0)


def dot_halves(left, right):
    high, low = split2(left)
    both = jnp.concatenate(
        [
            jnp.concatenate([high, high], axis=1),
            jnp.concatenate([low, jnp.zeros_like(low)], axis=1),
        ],
        axis=0,
    )
    out = jnp.dot(both, right, preferred_element_type=F32)
    return out[: left.shape[0]] + out[left.shape[0] :]


def dot3(left, right):
    return dot_halves(left, halves(right))


def compose(earlier, later, factors):
    out = dot3(earlier, later[:factors])
    return jnp.concatenate([out[:factors], out[factors:] + later[factors:]], axis=0)


def kernel(
    tms, sers,
    readings_in, present_in, loadings_in, prec_in, gain_in, frate_in, srate_in, regions_in,
    smoothed_ref, hist_ref,
    readings_ref, present_ref, loadings_ref, prec_ref, gain_ref, frate_ref, srate_ref, regions_ref,
    lt_s, sl_s, mem_s, score_s, send1, recv1, acc, recv2, cum, dmap, drecv, emaps, esend, smaps, ssend, lead_s,
    vin, vout, fown, fall, shown, shifts, table, hown, hall,
    ins, s1s, s1r, s2s, s2r, ds, dr, es, er, ss, sr, vs, vr, fs, fr, cs, cr, hs, hr,
):
    tm, ser = lax.axis_index("tm"), lax.axis_index("series")
    y, core = ser // 2, ser % 2
    ys = sers // 2
    local = readings_ref.shape[0]
    factors = loadings_ref.shape[1]
    rows = factors + 8
    hours = local // sers
    n = tms * sers
    me = tm * sers + ser
    pair, a = tm // 2, tm % 2
    pairs = tms // 2
    chips = 2 * ys
    g = a * ys + y

    barrier = pltpu.get_barrier_semaphore()

    plane = 2 * sers
    place_in = a * sers + ser

    def plane_peer(k):
        at = lax.rem(place_in + k, plane)
        return pair * 2 + at // sers, lax.rem(at, sers)

    for k in range(1, plane):
        pl.semaphore_signal(barrier, inc=1, device_id=plane_peer(k), device_id_type=MESH)
    inputs = [
        pltpu.make_async_copy(src, dst, ins.at[i])
        for i, (src, dst) in enumerate(
            [
                (loadings_in, loadings_ref), (prec_in, prec_ref), (present_in, present_ref),
                (readings_in, readings_ref), (gain_in, gain_ref), (frate_in, frate_ref),
                (srate_in, srate_ref), (regions_in, regions_ref),
            ]
        )
    ]

    @pl.when(pair > 0)
    def _():
        pl.semaphore_signal(barrier, inc=1, device_id=(tm - 2, ser), device_id_type=MESH)

    @pl.when(pair < pairs - 1)
    def _():
        pl.semaphore_signal(barrier, inc=1, device_id=(tm + 2, ser), device_id_type=MESH)

    for item in inputs:
        item.start()
    for item in inputs[:2]:
        item.wait()

    ltf = loadings_ref[...].astype(F32).T
    lt_s[...] = ltf.astype(BF16)
    sl_s[...] = (ltf * prec_ref[...]).T.astype(BF16)
    for item in inputs[2:4]:
        item.wait()
    present = present_ref[...].astype(F32)
    read_f = readings_ref[...].astype(F32)
    score_s[0:local] = jnp.dot(
        (read_f * present).astype(BF16), sl_s[...], preferred_element_type=F32
    )
    score_s[local:] = jnp.zeros_like(score_s[local:])

    half = factors // 2
    together_h = 2 if hours % 2 == 0 else 1
    sets = hours // together_h
    low_at = together_h * half

    def hour_terms(hour, dst):
        lower = []
        line = lax.broadcasted_iota(jnp.int32, (8, factors), 0)
        score = jnp.zeros((8, factors), F32)
        for j in range(together_h):
            mask = present_ref[pl.ds(hour + j, 1), :].astype(F32)
            mask = jnp.broadcast_to(mask, (16, mask.shape[1])).astype(BF16)
            left = lt_s[...].reshape(factors // 16, 16, mask.shape[1]) * mask[None]
            out = jnp.dot(
                left.reshape(factors, mask.shape[1]), sl_s[...], preferred_element_type=F32
            )
            dst[j * half : (j + 1) * half] = out[:half]
            lower.append(out[half:])
            row = jnp.broadcast_to(score_s[pl.ds(hour + j, 1), :], (8, factors))
            score = jnp.where(line == j, row, score)
        if together_h == 2:
            lane = lax.broadcasted_iota(jnp.int32, (half, factors), 1)
            dst[low_at : low_at + half] = jnp.where(
                lane >= half, lower[0], pltpu.roll(lower[1], half, 1)
            )
        else:
            dst[low_at : low_at + half] = lower[0]
        dst[low_at + half :] = score

    def unpack(packed, j):
        upper = packed[j * half : (j + 1) * half]
        lower = packed[low_at : low_at + half]
        right = lower[:, half:] if j == 0 else lower[:, :half]
        matrix = jnp.concatenate(
            [upper, jnp.concatenate([upper[:, half:].T, right], axis=1)], axis=0
        )
        first = lax.broadcasted_iota(jnp.int32, (8, factors), 0) == 0
        row = jnp.broadcast_to(packed[low_at + half + j : low_at + half + j + 1], (8, factors))
        return matrix, jnp.where(first, row, 0.0)

    def copy1(k, h):
        return pltpu.make_async_remote_copy(
            send1.at[k, h], recv1.at[k, h], s1s.at[k, h], s1r.at[k, h],
            device_id=(tm, y * 2 + (1 - core)), device_id_type=MESH,
        )

    def copy2(k, h):
        return pltpu.make_async_remote_copy(
            acc.at[k, h], recv2.at[k, h], s2s.at[k, h], s2r.at[k, h],
            device_id=(tm, lax.rem(y + k, ys) * 2 + core), device_id_type=MESH,
        )

    order = list(range(1, ys)) + [0]
    for place, k in enumerate(order):
        owner = lax.rem(y + k, ys) * 2
        for h in range(sets):
            hour_terms((owner + (1 - core)) * hours + h * together_h, send1.at[k, h])
            if place == 0 and h == 0:
                before = jnp.where(pair > 0, 1, 0)
                behind = jnp.where(pair < pairs - 1, 1, 0)
                pl.semaphore_wait(barrier, plane - 1 + before + behind)
            copy1(k, h).start()
        for h in range(sets):
            hour_terms((owner + core) * hours + h * together_h, acc.at[k, h])
            if k:
                copy1(k, h).wait_recv()
                acc[k, h] = acc[k, h] + recv1[k, h]
                copy2(k, h).start()

    for item in inputs[4:]:
        item.wait()
    wide = lax.broadcasted_iota(jnp.int32, (factors, regions_ref.shape[1]), 0) % GROUPS
    mem_s[...] = jnp.where(wide == regions_ref[...], 1.0, 0.0).astype(F32).T.astype(BF16)
    gain = gain_ref[...]
    decays = jnp.exp(-frate_ref[...])
    srate = srate_ref[...]
    retain = jnp.exp(-srate)
    keep = 1.0 - retain * decays
    eye = (
        lax.broadcasted_iota(jnp.int32, (factors, factors), 0)
        == lax.broadcasted_iota(jnp.int32, (factors, factors), 1)
    )
    eye_f = jnp.where(eye, 1.0, 0.0).astype(F32)
    decay_col = jnp.sum(jnp.where(eye, decays, 0.0), axis=1, keepdims=True)
    for h in range(sets):
        copy1(0, h).wait_recv()

    maps = []
    for h in range(sets):
        total = acc[0, h] + recv1[0, h]
        for k in range(1, ys):
            copy2(k, h).wait_recv()
            total = total + recv2[k, h]
        for j in range(together_h):
            inform, scores = unpack(total, j)
            maps.append(
                jnp.concatenate([decay_col * (eye_f - gain * inform), gain * scores], axis=0)
            )
    step = 1
    while step < hours:
        maps = [
            compose(maps[h - step], maps[h], factors) if h >= step else maps[h]
            for h in range(hours)
        ]
        step *= 2
    dmap[0] = maps[-1]
    adds = keep * maps[0]
    for h in range(1, hours):
        adds = adds + keep * jnp.exp(-float(h) * srate) * maps[h]
    dmap[1] = adds
    dcopy = pltpu.make_async_remote_copy(
        dmap, drecv, ds, dr, device_id=(tm, y * 2 + (1 - core)), device_id_type=MESH
    )
    dcopy.start()
    for h in range(hours):
        cum[:, h * factors : (h + 1) * factors] = maps[h]
    dcopy.wait_recv()
    mine, other = dmap[0], drecv[0]
    leads = core == 0
    whole = compose(jnp.where(leads, mine, other), jnp.where(leads, other, mine), factors)
    esend[...] = whole

    def ecopy(k):
        to = lax.rem(g + k, chips)
        return pltpu.make_async_remote_copy(
            esend, emaps.at[k], es.at[k], er.at[k],
            device_id=(pair * 2 + to // ys, lax.rem(to, ys) * 2 + core), device_id_type=MESH,
        )

    for k in range(1, chips):
        ecopy(k).start()
    emaps[0] = whole
    first = jnp.where(leads, mine, other)
    mine_adds, other_adds = dmap[1], drecv[1]
    chip_adds = jnp.where(leads, mine_adds, other_adds) + jnp.exp(-float(hours) * srate) * compose(
        first, jnp.where(leads, other_adds, mine_adds), factors
    )
    ssend[...] = chip_adds

    def scopy(k):
        to = lax.rem(g + k, chips)
        return pltpu.make_async_remote_copy(
            ssend, smaps.at[k], ss.at[k], sr.at[k],
            device_id=(pair * 2 + to // ys, lax.rem(to, ys) * 2 + core), device_id_type=MESH,
        )

    for k in range(1, chips):
        scopy(k).start()
    smaps[0] = chip_adds
    span = 2 * local
    after = (a + 1) * local
    hour_at = (
        lax.broadcasted_iota(jnp.int32, (plane, hours, factors), 0) * hours
        + lax.broadcasted_iota(jnp.int32, (plane, hours, factors), 1)
    )
    far = (hour_at - after).astype(F32)
    tail_w = jnp.where(far >= 0.0, keep[None] * jnp.exp(-jnp.maximum(far, 0.0) * srate[None]), 0.0)
    end_w = jnp.exp(-(span - after).astype(F32) * srate)
    span_w = jnp.exp(-float(span) * srate)
    for k in range(1, chips):
        ecopy(k).wait_recv()
    parts = [emaps[lax.rem(g - at + chips, chips)] for at in range(chips)]
    level = parts
    while len(level) > 1:
        level = [
            compose(level[i], level[i + 1], factors) if i + 1 < len(level) else level[i]
            for i in range(0, len(level), 2)
        ]
    total = level[0]

    vcopy = pltpu.make_async_remote_copy(
        vout, vin, vs, vr,
        device_id=(lax.rem(tm + 2, tms), ser), device_id_type=MESH,
    )

    @pl.when(pair == 0)
    def _():
        vin[...] = jnp.zeros_like(vin)
        vout[...] = total[factors:]
        vcopy.start()

    total_h = halves(total[:factors])

    def forward():
        vcopy.wait_recv()

        @pl.when(pair < pairs - 1)
        def _():
            vout[...] = dot_halves(vin[...], total_h) + total[factors:]
            vcopy.start()

    @pl.when(pair == 1)
    def _():
        forward()

    unit = jnp.concatenate([eye_f, jnp.zeros((8, factors), F32)], axis=0)
    start_map = unit
    before_chip = [parts[0]]
    for at in range(1, chips):
        start_map = jnp.where(g == at, before_chip[-1], start_map)
        if at + 1 < chips:
            before_chip.append(compose(before_chip[-1], parts[at], factors))
    start_map = jnp.where(leads, start_map, compose(start_map, other, factors))
    cums = cum[...]
    lead = dot3(start_map, cums[:factors])
    wide_at = hours * factors
    lead_s[:, :wide_at] = halves(lead[:factors])
    lead_b = lead[factors:] + cums[factors:]
    at_end = pair == pairs - 1
    for k in range(1, chips):
        scopy(k).wait_recv()
    group_adds = smaps[lax.rem(g, chips)] + jnp.where(at_end, span_w * decays, 0.0) * total
    for at in range(1, chips):
        group_adds = group_adds + jnp.exp(-float(2 * hours * at) * srate) * compose(
            before_chip[at - 1], smaps[lax.rem(g - at + chips, chips)], factors
        )
    lead_s[:, wide_at:] = halves(group_adds[:factors])
    lead_b = jnp.concatenate([lead_b, group_adds[factors:]], axis=1)

    @pl.when(pair > 1)
    def _():
        forward()

    current = vin[...]
    filtered = dot_halves(current, lead_s[...]) + lead_b
    for h in range(hours):
        row = filtered[0:1, h * factors : (h + 1) * factors]
        fown[h : h + 1, :] = row
    shown[...] = filtered[:, hours * factors :]

    def ccopy(to, of):
        return pltpu.make_async_remote_copy(
            shown, shifts.at[of], cs.at[to], cr.at[of],
            device_id=(to * 2 + a, ser), device_id_type=MESH,
        )

    @pl.loop(0, pair)
    def _(to):
        ccopy(to, pair).start()

    fall[place_in] = fown[...]

    def fcopy(k):
        return pltpu.make_async_remote_copy(
            fown, fall.at[place_in], fs.at[k], fr.at[k],
            device_id=plane_peer(k), device_id_type=MESH,
        )

    for k in range(1, plane):
        fcopy(k).start()
    prec_root = jnp.sqrt(prec_ref[...])
    for k in range(1, plane):
        fcopy(k).wait_recv()
    together = fall[...]
    ending = decays * together[plane - 1][hours - 1 : hours]
    follow = jnp.sum(jnp.sum(together * tail_w, axis=0), axis=0, keepdims=True)

    def gather(of, held):
        total, weight = held
        ccopy(pair, of).wait_recv()
        return total + weight * shifts[of][0:1], weight * span_w

    beyond, _ = lax.fori_loop(
        pair + 1, pairs, gather, (jnp.where(at_end, ending, 0.0), jnp.ones_like(span_w))
    )
    follow = follow + end_w * beyond
    for s in range(sers - 1, -1, -1):
        block = fall[a * sers + s]
        for h in range(hours - 1, -1, -1):
            follow = keep * block[h : h + 1] + retain * follow
            smoothed_ref[s * hours + h : s * hours + h + 1, :] = follow

    fitted = jnp.dot(smoothed_ref[...].astype(BF16), lt_s[...], preferred_element_type=F32)
    standard = (readings_ref[...].astype(F32) - fitted) * prec_root
    probab = 0.5 * (1.0 + lax.erf(standard * 0.7071067811865476))
    spot = jnp.where(present_ref[...] > 0, probab * BINS - 0.5, -4.0)
    for b in range(BINS):
        table[b : b + 1, :] = jnp.sum(
            jnp.maximum(0.0, 1.0 - jnp.abs(spot - b)), axis=0, keepdims=True
        )
    padded = table.shape[0]
    if padded > BINS:
        table[BINS:, :] = jnp.zeros_like(table[BINS:, :])
    th, tl = split2(table[...])
    tally = jnp.dot(
        jnp.concatenate([th, tl], axis=0), mem_s[...], preferred_element_type=F32
    )
    tally = tally[:padded] + tally[padded:]
    lane = lax.broadcasted_iota(jnp.int32, tally.shape, 1) // GROUPS
    sub = lax.broadcasted_iota(jnp.int32, tally.shape, 0) % 8
    tally = jnp.where(lane == sub, tally, 0.0).reshape(padded // 8, 8, tally.shape[1])
    hown[...] = jnp.zeros_like(hown)
    hown[0 : padded // 8, :] = jnp.sum(tally, axis=1)
    hall[me] = hown[...]

    @pl.loop(1, n)
    def _(k):
        peer = lax.rem(me + k, n)
        pltpu.make_async_remote_copy(
            hown, hall.at[me], hs, hr,
            device_id=(peer // sers, lax.rem(peer, sers)), device_id_type=MESH,
        ).start()

    for k in range(ys):
        for h in range(sets):
            copy1(k, h).wait_send()
            if k:
                copy2(k, h).wait_send()
    dcopy.wait_send()
    for k in range(1, chips):
        ecopy(k).wait_send()
        scopy(k).wait_send()

    @pl.when(pair < pairs - 1)
    def _():
        vcopy.wait_send()

    for k in range(1, plane):
        fcopy(k).wait_send()

    @pl.loop(0, pair)
    def _(to):
        ccopy(to, pair).wait_send()

    hdrain = pltpu.make_async_remote_copy(
        hall.at[pl.ds(0, n - 1)], hall.at[pl.ds(0, n - 1)], hs, hr,
        device_id=(tm, lax.rem(ser + 1, sers)), device_id_type=MESH,
    )
    hdrain.wait_recv()
    hdrain.wait_send()
    hist_ref[...] = jnp.sum(hall[...], axis=0)


def solution(mesh):
    tms, sers = mesh.shape["tm"], mesh.shape["series"]

    def body(readings, present, loadings, prec, gain, frate, srate, regions):
        local, series = readings.shape
        factors = loadings.shape[1]
        hours = local // sers
        n, ys = tms * sers, sers // 2
        chips = 2 * ys
        rows = factors + 8
        padded = -(-BINS // 8) * 8
        together = 2 if hours % 2 == 0 else 1
        sets, packed_rows = hours // together, (together + 1) * (factors // 2) + 8
        vm = pltpu.VMEM
        dma = pltpu.SemaphoreType.DMA
        smoothed, packed = pl.pallas_call(
            functools.partial(kernel, tms, sers),
            out_shape=(
                vm((local, factors), F32),
                vm((4, 8 * GROUPS), F32),
            ),
            in_specs=[pl.BlockSpec(memory_space=pl.ANY)] * 8,
            out_specs=(pl.BlockSpec(memory_space=vm),) * 2,
            scratch_shapes=[
                vm((local, series), readings.dtype),
                vm((local, series), present.dtype),
                vm((series, factors), loadings.dtype),
                vm((1, series), F32),
                vm((1, factors), F32),
                vm((1, factors), F32),
                vm((1, factors), F32),
                vm((1, series), regions.dtype),
                vm((factors, series), BF16),
                vm((series, factors), BF16),
                vm((series, 8 * GROUPS), BF16),
                vm((local + 8, factors), F32),
                vm((ys, sets, packed_rows, factors), F32),
                vm((ys, sets, packed_rows, factors), F32),
                vm((ys, sets, packed_rows, factors), F32),
                vm((ys, sets, packed_rows, factors), F32),
                vm((rows, hours * factors), F32),
                vm((2, rows, factors), F32),
                vm((2, rows, factors), F32),
                vm((chips, rows, factors), F32),
                vm((rows, factors), F32),
                vm((chips, rows, factors), F32),
                vm((rows, factors), F32),
                vm((2 * factors, (hours + 1) * factors), BF16),
                vm((8, factors), F32),
                vm((8, factors), F32),
                vm((hours, factors), F32),
                vm((2 * sers, hours, factors), F32),
                vm((8, factors), F32),
                vm((tms // 2, 8, factors), F32),
                vm((padded, series), F32),
                vm((4, 8 * GROUPS), F32),
                vm((n, 4, 8 * GROUPS), F32),
                dma((8,)),
                dma((ys, sets)),
                dma((ys, sets)),
                dma((ys, sets)),
                dma((ys, sets)),
                dma, dma,
                dma((chips,)),
                dma((chips,)),
                dma((chips,)),
                dma((chips,)),
                dma, dma,
                dma((2 * sers,)),
                dma((2 * sers,)),
                dma((tms // 2,)),
                dma((tms // 2,)),
                dma, dma,
            ],
            compiler_params=pltpu.CompilerParams(collective_id=0, has_side_effects=True),
        )(
            readings, present, loadings, prec.reshape(1, -1), gain.reshape(1, -1),
            frate.reshape(1, -1), srate.reshape(1, -1), regions.reshape(1, -1),
        )
        scale = BINS * GROUPS / (local * tms * series * sers)
        histogram = packed.reshape(-1, GROUPS)[:BINS].T * scale
        return smoothed, histogram

    in_specs = (
        P("tm", "series"), P("tm", "series"), P("series", None), P("series"),
        P(), P(), P(), P("series"),
    )
    return jax.shard_map(
        body, mesh=mesh, in_specs=in_specs, out_specs=(P("tm", None), P()), check_vma=False
    )
```

profile of v0, /device:TPU:0, one launch (start us, length us, event | category | flops | bytes accessed | tf_op | source)
XLA Modules:
  0.0 38.6 jit_solution(12548047883380120014)
XLA Ops:
  0.6 36.6 %shard_map.95 = (f32[16,128]{1,0:T(8,128)S(1)}, f32[4,128]{1,0:T(4,128)S(1)}) custom-call(bf16[16,1024]{1,0:T(8,128)(2,1)} %readings_in.1, s32[16,1024]{1,0:T(8,128)} %present_in.1, bf16[1024,128]{1,0:T(8,128)(2,1)} %loadings_in.1, f32[1,1024]{1,0:T(1,128)} %bitcast.7, f32[1,128]{1,0:T(1,128)} %bitcast.9, f32[1,128]{1,0:T(1,128)} %bitcast.10, ...), custom_call_target="tpu_custom_call" | custom-call | tf_op jit(solution)/shard_map/pallas_call | solution.py:467
  37.3 0.6 %copy.13 = f32[16,128]{1,0:T(8,128)} copy(f32[16,128]{1,0:T(8,128)S(1)} %get-tuple-element.8) | data formatting | bytes 16384
  37.9 0.1 reshape.27
  38.0 0.7 %copy.11 = f32[16,20]{1,0:T(8,128)} copy(f32[16,20]{0,1:T(8,128)S(1)} %fusion) | data formatting | bytes 2560
  (1 shorter events, 0.0 us)
where the time goes:
time: 38.8 us; the launch traced here: 38.6 us
  Pallas kernels  36.6 us (94%)
  local copies, waits for them, and re-layouts  1.36 us (4%)
  between operations  0.64 us (2%)
    pallas_call x1, Pallas kernels, body(): pl.pallas_call(functools.partial(kernel, tms, sers), out_shape=(vm((local...  36.6 us
    unnamed x2, local copies, waits for them, and re-layouts  1.28 us

commit v1 on v0

--- a/solution.py
+++ b/solution.py
@@ -52,8 +52,8 @@
     smoothed_ref, hist_ref,
     readings_ref, present_ref, loadings_ref, prec_ref, gain_ref, frate_ref, srate_ref, regions_ref,
     lt_s, sl_s, mem_s, score_s, send1, recv1, acc, recv2, cum, dmap, drecv, emaps, esend, smaps, ssend, lead_s,
-    vin, vout, fown, fall, shown, shifts, table, hown, hall,
-    ins, s1s, s1r, s2s, s2r, ds, dr, es, er, ss, sr, vs, vr, fs, fr, cs, cr, hs, hr,
+    vin, vout, vcur, tsend, trecv, fown, fall, shown, shifts, table, hown, hall,
+    ins, s1s, s1r, s2s, s2r, ds, dr, es, er, ss, sr, vs, vr, ts, tr, fs, fr, cs, cr, hs, hr,
 ):
     tm, ser = lax.axis_index("tm"), lax.axis_index("series")
     y, core = ser // 2, ser % 2
@@ -98,6 +98,14 @@
     @pl.when(pair < pairs - 1)
     def _():
         pl.semaphore_signal(barrier, inc=1, device_id=(tm + 2, ser), device_id_type=MESH)
+
+    @pl.when(pair > 1)
+    def _():
+        pl.semaphore_signal(barrier, inc=1, device_id=(tm - 4, ser), device_id_type=MESH)
+
+    @pl.when(pair < pairs - 2)
+    def _():
+        pl.semaphore_signal(barrier, inc=1, device_id=(tm + 4, ser), device_id_type=MESH)
 
     for item in inputs:
         item.start()
@@ -174,8 +182,8 @@
         for h in range(sets):
             hour_terms((owner + (1 - core)) * hours + h * together_h, send1.at[k, h])
             if place == 0 and h == 0:
-                before = jnp.where(pair > 0, 1, 0)
-                behind = jnp.where(pair < pairs - 1, 1, 0)
+                before = jnp.where(pair > 0, 1, 0) + jnp.where(pair > 1, 1, 0)
+                behind = jnp.where(pair < pairs - 1, 1, 0) + jnp.where(pair < pairs - 2, 1, 0)
                 pl.semaphore_wait(barrier, plane - 1 + before + behind)
             copy1(k, h).start()
         for h in range(sets):
@@ -286,26 +294,50 @@
         ]
     total = level[0]
 
-    vcopy = pltpu.make_async_remote_copy(
-        vout, vin, vs, vr,
-        device_id=(lax.rem(tm + 2, tms), ser), device_id_type=MESH,
-    )
+    def vcopy(far):
+        return pltpu.make_async_remote_copy(
+            vout, vin, vs.at[far - 1], vr,
+            device_id=(lax.rem(tm + 2 * far, tms), ser), device_id_type=MESH,
+        )
+
+    tcopy = pltpu.make_async_remote_copy(
+        tsend, trecv, ts, tr, device_id=(lax.rem(tm + 2, tms), ser), device_id_type=MESH
+    )
+    odd = pair % 2 == 1
+    hands_map = (pair % 2 == 0) & (pair > 0) & (pair < pairs - 1)
+
+    @pl.when(hands_map)
+    def _():
+        tsend[...] = total
+        tcopy.start()
 
     @pl.when(pair == 0)
     def _():
-        vin[...] = jnp.zeros_like(vin)
-        vout[...] = total[factors:]
-        vcopy.start()
-
-    total_h = halves(total[:factors])
+        vcur[...] = jnp.zeros_like(vcur)
+        vout[...] = total[factors : factors + 1]
+        vcopy(1).start()
+
+    def carry(vector, matrix, shift):
+        column = jnp.sum(jnp.where(eye, vector, 0.0), axis=1, keepdims=True)
+        return jnp.sum(column * matrix, axis=0, keepdims=True) + shift
 
     def forward():
-        vcopy.wait_recv()
-
-        @pl.when(pair < pairs - 1)
+        vcopy(1).wait_recv()
+        vcur[...] = vin[...]
+
+        @pl.when(odd & (pair > 1))
         def _():
-            vout[...] = dot_halves(vin[...], total_h) + total[factors:]
-            vcopy.start()
+            tcopy.wait_recv()
+            vcur[...] = carry(vin[...], trecv[0:factors], trecv[factors : factors + 1])
+
+        @pl.when(odd & (pair < pairs - 1))
+        def _():
+            vout[...] = carry(vcur[...], total[:factors], total[factors : factors + 1])
+            vcopy(1).start()
+
+            @pl.when(pair < pairs - 2)
+            def _():
+                vcopy(2).start()
 
     @pl.when(pair == 1)
     def _():
@@ -339,7 +371,7 @@
     def _():
         forward()
 
-    current = vin[...]
+    current = jnp.broadcast_to(vcur[...], (8, factors))
     filtered = dot_halves(current, lead_s[...]) + lead_b
     for h in range(hours):
         row = filtered[0:1, h * factors : (h + 1) * factors]
@@ -407,17 +439,22 @@
     lane = lax.broadcasted_iota(jnp.int32, tally.shape, 1) // GROUPS
     sub = lax.broadcasted_iota(jnp.int32, tally.shape, 0) % 8
     tally = jnp.where(lane == sub, tally, 0.0).reshape(padded // 8, 8, tally.shape[1])
-    hown[...] = jnp.zeros_like(hown)
-    hown[0 : padded // 8, :] = jnp.sum(tally, axis=1)
+    hown[...] = jnp.sum(tally, axis=1)
     hall[me] = hown[...]
 
-    @pl.loop(1, n)
-    def _(k):
-        peer = lax.rem(me + k, n)
+    def hsend(k):
+        at = lax.rem(place_in + (plane - 1 - k % plane), plane)
+        to = lax.rem(pair + (pairs - 1 - k // plane), pairs)
         pltpu.make_async_remote_copy(
             hown, hall.at[me], hs, hr,
-            device_id=(peer // sers, lax.rem(peer, sers)), device_id_type=MESH,
+            device_id=(to * 2 + at // sers, lax.rem(at, sers)), device_id_type=MESH,
         ).start()
+
+    if n <= 64:
+        for k in range(n - 1):
+            hsend(k)
+    else:
+        pl.loop(0, n - 1)(hsend)
 
     for k in range(ys):
         for h in range(sets):
@@ -429,9 +466,17 @@
         ecopy(k).wait_send()
         scopy(k).wait_send()
 
-    @pl.when(pair < pairs - 1)
-    def _():
-        vcopy.wait_send()
+    @pl.when((odd | (pair == 0)) & (pair < pairs - 1))
+    def _():
+        vcopy(1).wait_send()
+
+    @pl.when(odd & (pair < pairs - 2))
+    def _():
+        vcopy(2).wait_send()
+
+    @pl.when(hands_map)
+    def _():
+        tcopy.wait_send()
 
     for k in range(1, plane):
         fcopy(k).wait_send()
@@ -468,7 +513,7 @@
             functools.partial(kernel, tms, sers),
             out_shape=(
                 vm((local, factors), F32),
-                vm((4, 8 * GROUPS), F32),
+                vm((padded // 8, 8 * GROUPS), F32),
             ),
             in_specs=[pl.BlockSpec(memory_space=pl.ANY)] * 8,
             out_specs=(pl.BlockSpec(memory_space=vm),) * 2,
@@ -497,15 +542,18 @@
                 vm((chips, rows, factors), F32),
                 vm((rows, factors), F32),
                 vm((2 * factors, (hours + 1) * factors), BF16),
-                vm((8, factors), F32),
-                vm((8, factors), F32),
+                vm((1, factors), F32),
+                vm((1, factors), F32),
+                vm((1, factors), F32),
+                vm((rows, factors), F32),
+                vm((rows, factors), F32),
                 vm((hours, factors), F32),
                 vm((2 * sers, hours, factors), F32),
                 vm((8, factors), F32),
                 vm((tms // 2, 8, factors), F32),
                 vm((padded, series), F32),
-                vm((4, 8 * GROUPS), F32),
-                vm((n, 4, 8 * GROUPS), F32),
+                vm((padded // 8, 8 * GROUPS), F32),
+                vm((n, padded // 8, 8 * GROUPS), F32),
                 dma((8,)),
                 dma((ys, sets)),
                 dma((ys, sets)),
@@ -516,7 +564,7 @@
                 dma((chips,)),
                 dma((chips,)),
                 dma((chips,)),
-                dma, dma,
+                dma((2,)), dma, dma, dma,
                 dma((2 * sers,)),
                 dma((2 * sers,)),
                 dma((tms // 2,)),

time: 38.8 us -> 37.9 us (0.977)
  Pallas kernels: 36.6 us -> 35.7 us
    pallas_call x1, Pallas kernels: 36.6 us -> 35.7 us  [body(): pl.pallas_call(functools.partial(kernel, tms, sers), out_shape=(vm((local...]
where the time goes in v1:
time: 37.9 us; the launch traced here: 37.7 us
  Pallas kernels  35.7 us (94%)
  local copies, waits for them, and re-layouts  1.36 us (4%)
  between operations  0.64 us (2%)
    pallas_call x1, Pallas kernels, body(): pl.pallas_call(functools.partial(kernel, tms, sers), out_shape=(vm((local...  35.7 us
    unnamed x2, local copies, waits for them, and re-layouts  1.28 us

profile of v1, /device:TPU:0, one launch (start us, length us, event | category | flops | bytes accessed | tf_op | source)
XLA Modules:
  0.0 37.7 jit_solution(17955412174475337026)
XLA Ops:
  0.6 35.7 %shard_map.95 = (f32[16,128]{1,0:T(8,128)S(1)}, f32[3,128]{1,0:T(4,128)S(1)}) custom-call(bf16[16,1024]{1,0:T(8,128)(2,1)} %readings_in.1, s32[16,1024]{1,0:T(8,128)} %present_in.1, bf16[1024,128]{1,0:T(8,128)(2,1)} %loadings_in.1, f32[1,1024]{1,0:T(1,128)} %bitcast.7, f32[1,128]{1,0:T(1,128)} %bitcast.9, f32[1,128]{1,0:T(1,128)} %bitcast.10, ...), custom_call_target="tpu_custom_call" | custom-call | tf_op jit(solution)/shard_map/pallas_call | solution.py:512
  36.4 0.6 %copy.13 = f32[16,128]{1,0:T(8,128)} copy(f32[16,128]{1,0:T(8,128)S(1)} %get-tuple-element.8) | data formatting | bytes 16384
  37.0 0.1 reshape.27
  37.1 0.7 %copy.11 = f32[16,20]{1,0:T(8,128)} copy(f32[16,20]{0,1:T(8,128)S(1)} %fusion) | data formatting | bytes 2560
  (1 shorter events, 0.0 us)

commit v2 on v1

--- a/solution.py
+++ b/solution.py
@@ -52,8 +52,8 @@
     smoothed_ref, hist_ref,
     readings_ref, present_ref, loadings_ref, prec_ref, gain_ref, frate_ref, srate_ref, regions_ref,
     lt_s, sl_s, mem_s, score_s, send1, recv1, acc, recv2, cum, dmap, drecv, emaps, esend, smaps, ssend, lead_s,
-    vin, vout, vcur, tsend, trecv, fown, fall, shown, shifts, table, hown, hall,
-    ins, s1s, s1r, s2s, s2r, ds, dr, es, er, ss, sr, vs, vr, ts, tr, fs, fr, cs, cr, hs, hr,
+    vin, vout, vcur, bin_s, tsend, trecv, fown, fall, shown, shifts, table, hown, hall,
+    ins, s1s, s1r, s2s, s2r, ds, dr, es, er, ss, sr, vs, vr, vls, bs, br, ts, tr, fs, fr, cs, cr, hs, hr,
 ):
     tm, ser = lax.axis_index("tm"), lax.axis_index("series")
     y, core = ser // 2, ser % 2
@@ -68,18 +68,8 @@
     pairs = tms // 2
     chips = 2 * ys
     g = a * ys + y
-
-    barrier = pltpu.get_barrier_semaphore()
-
-    plane = 2 * sers
-    place_in = a * sers + ser
-
-    def plane_peer(k):
-        at = lax.rem(place_in + k, plane)
-        return pair * 2 + at // sers, lax.rem(at, sers)
-
-    for k in range(1, plane):
-        pl.semaphore_signal(barrier, inc=1, device_id=plane_peer(k), device_id_type=MESH)
+    leader = (pair == 0) & (g == chips - 1)
+
     inputs = [
         pltpu.make_async_copy(src, dst, ins.at[i])
         for i, (src, dst) in enumerate(
@@ -90,25 +80,42 @@
             ]
         )
     ]
-
-    @pl.when(pair > 0)
-    def _():
-        pl.semaphore_signal(barrier, inc=1, device_id=(tm - 2, ser), device_id_type=MESH)
-
-    @pl.when(pair < pairs - 1)
-    def _():
-        pl.semaphore_signal(barrier, inc=1, device_id=(tm + 2, ser), device_id_type=MESH)
-
-    @pl.when(pair > 1)
-    def _():
-        pl.semaphore_signal(barrier, inc=1, device_id=(tm - 4, ser), device_id_type=MESH)
-
-    @pl.when(pair < pairs - 2)
-    def _():
-        pl.semaphore_signal(barrier, inc=1, device_id=(tm + 4, ser), device_id_type=MESH)
-
     for item in inputs:
         item.start()
+
+    barrier = pltpu.get_barrier_semaphore()
+
+    plane = 2 * sers
+    place_in = a * sers + ser
+
+    def plane_peer(k):
+        at = lax.rem(place_in + k, plane)
+        return pair * 2 + at // sers, lax.rem(at, sers)
+
+    for k in range(1, plane):
+        pl.semaphore_signal(barrier, inc=1, device_id=plane_peer(k), device_id_type=MESH)
+    @pl.when(pair > 0)
+    def _():
+        pl.semaphore_signal(barrier, inc=1, device_id=(tm - 2, ser), device_id_type=MESH)
+
+    @pl.when(pair < pairs - 1)
+    def _():
+        pl.semaphore_signal(barrier, inc=1, device_id=(tm + 2, ser), device_id_type=MESH)
+
+    @pl.when(pair > 1)
+    def _():
+        pl.semaphore_signal(barrier, inc=1, device_id=(tm - 4, ser), device_id_type=MESH)
+
+    @pl.when(pair < pairs - 2)
+    def _():
+        pl.semaphore_signal(barrier, inc=1, device_id=(tm + 4, ser), device_id_type=MESH)
+
+    @pl.when((pair == 1) & (g < chips - 1))
+    def _():
+        pl.semaphore_signal(
+            barrier, inc=1, device_id=(1, (ys - 1) * 2 + core), device_id_type=MESH
+        )
+
     for item in inputs[:2]:
         item.wait()
 
@@ -124,45 +131,53 @@
     )
     score_s[local:] = jnp.zeros_like(score_s[local:])
 
-    half = factors // 2
     together_h = 2 if hours % 2 == 0 else 1
     sets = hours // together_h
-    low_at = together_h * half
-
-    def hour_terms(hour, dst):
-        lower = []
-        line = lax.broadcasted_iota(jnp.int32, (8, factors), 0)
-        score = jnp.zeros((8, factors), F32)
-        for j in range(together_h):
-            mask = present_ref[pl.ds(hour + j, 1), :].astype(F32)
+    sub = lax.broadcasted_iota(jnp.int32, (factors, factors), 0)
+    lane = lax.broadcasted_iota(jnp.int32, (factors, factors), 1)
+    eye = sub == lane
+    upper = lane > sub
+    line = lax.broadcasted_iota(jnp.int32, (8, factors), 0)
+
+    def hour_terms(base, dst):
+        lefts = []
+        for j in range(hours):
+            mask = present_ref[pl.ds(base + j, 1), :].astype(F32)
             mask = jnp.broadcast_to(mask, (16, mask.shape[1])).astype(BF16)
             left = lt_s[...].reshape(factors // 16, 16, mask.shape[1]) * mask[None]
-            out = jnp.dot(
-                left.reshape(factors, mask.shape[1]), sl_s[...], preferred_element_type=F32
-            )
-            dst[j * half : (j + 1) * half] = out[:half]
-            lower.append(out[half:])
-            row = jnp.broadcast_to(score_s[pl.ds(hour + j, 1), :], (8, factors))
-            score = jnp.where(line == j, row, score)
-        if together_h == 2:
-            lane = lax.broadcasted_iota(jnp.int32, (half, factors), 1)
-            dst[low_at : low_at + half] = jnp.where(
-                lane >= half, lower[0], pltpu.roll(lower[1], half, 1)
-            )
+            lefts.append(left.reshape(factors, mask.shape[1]))
+        out = jnp.dot(
+            jnp.concatenate(lefts, axis=0), sl_s[...], preferred_element_type=F32
+        )
+        for h in range(sets):
+            at = h * together_h
+            first = out[at * factors : (at + 1) * factors]
+            tail = jnp.zeros((8, factors), F32)
+            if together_h == 2:
+                second = out[(at + 1) * factors : (at + 2) * factors]
+                dst[h, :factors] = jnp.where(upper, first, second)
+                corner = jnp.sum(jnp.where(eye, first, 0.0), axis=0, keepdims=True)
+                tail = jnp.where(line == together_h, corner, tail)
+            else:
+                dst[h, :factors] = first
+            for j in range(together_h):
+                row = jnp.broadcast_to(score_s[pl.ds(base + at + j, 1), :], (8, factors))
+                tail = jnp.where(line == j, row, tail)
+            dst[h, factors:] = tail
+
+    def unpack(packed):
+        block, tail = packed[:factors], packed[factors:]
+        if together_h == 1:
+            matrices = [block]
         else:
-            dst[low_at : low_at + half] = lower[0]
-        dst[low_at + half :] = score
-
-    def unpack(packed, j):
-        upper = packed[j * half : (j + 1) * half]
-        lower = packed[low_at : low_at + half]
-        right = lower[:, half:] if j == 0 else lower[:, :half]
-        matrix = jnp.concatenate(
-            [upper, jnp.concatenate([upper[:, half:].T, right], axis=1)], axis=0
-        )
-        first = lax.broadcasted_iota(jnp.int32, (8, factors), 0) == 0
-        row = jnp.broadcast_to(packed[low_at + half + j : low_at + half + j + 1], (8, factors))
-        return matrix, jnp.where(first, row, 0.0)
+            turned = block.T
+            matrices = [
+                jnp.where(eye, tail[together_h : together_h + 1], jnp.where(upper, block, turned)),
+                jnp.where(upper, turned, block),
+            ]
+        return [
+            (matrices[j], jnp.where(line == 0, tail[j : j + 1], 0.0)) for j in range(together_h)
+        ]
 
     def copy1(k, h):
         return pltpu.make_async_remote_copy(
@@ -179,16 +194,17 @@
     order = list(range(1, ys)) + [0]
     for place, k in enumerate(order):
         owner = lax.rem(y + k, ys) * 2
+        hour_terms((owner + (1 - core)) * hours, send1.at[k])
+        if place == 0:
+            before = jnp.where(pair > 0, 1, 0) + jnp.where(pair > 1, 1, 0)
+            behind = jnp.where(pair < pairs - 1, 1, 0) + jnp.where(pair < pairs - 2, 1, 0)
+            extra = jnp.where(leader, chips - 1, 0)
+            pl.semaphore_wait(barrier, plane - 1 + before + behind + extra)
         for h in range(sets):
-            hour_terms((owner + (1 - core)) * hours + h * together_h, send1.at[k, h])
-            if place == 0 and h == 0:
-                before = jnp.where(pair > 0, 1, 0) + jnp.where(pair > 1, 1, 0)
-                behind = jnp.where(pair < pairs - 1, 1, 0) + jnp.where(pair < pairs - 2, 1, 0)
-                pl.semaphore_wait(barrier, plane - 1 + before + behind)
             copy1(k, h).start()
-        for h in range(sets):
-            hour_terms((owner + core) * hours + h * together_h, acc.at[k, h])
-            if k:
+        hour_terms((owner + core) * hours, acc.at[k])
+        if k:
+            for h in range(sets):
                 copy1(k, h).wait_recv()
                 acc[k, h] = acc[k, h] + recv1[k, h]
                 copy2(k, h).start()
@@ -202,10 +218,6 @@
     srate = srate_ref[...]
     retain = jnp.exp(-srate)
     keep = 1.0 - retain * decays
-    eye = (
-        lax.broadcasted_iota(jnp.int32, (factors, factors), 0)
-        == lax.broadcasted_iota(jnp.int32, (factors, factors), 1)
-    )
     eye_f = jnp.where(eye, 1.0, 0.0).astype(F32)
     decay_col = jnp.sum(jnp.where(eye, decays, 0.0), axis=1, keepdims=True)
     for h in range(sets):
@@ -217,61 +229,79 @@
         for k in range(1, ys):
             copy2(k, h).wait_recv()
             total = total + recv2[k, h]
-        for j in range(together_h):
-            inform, scores = unpack(total, j)
-            maps.append(
-                jnp.concatenate([decay_col * (eye_f - gain * inform), gain * scores], axis=0)
-            )
-    step = 1
-    while step < hours:
-        maps = [
-            compose(maps[h - step], maps[h], factors) if h >= step else maps[h]
-            for h in range(hours)
+        fresh = [
+            jnp.concatenate([decay_col * (eye_f - gain * inform), gain * scores], axis=0)
+            for inform, scores in unpack(total)
         ]
-        step *= 2
+        if together_h == 2:
+            fresh[1] = compose(fresh[0], fresh[1], factors)
+        if maps:
+            fresh = [compose(maps[-1], item, factors) for item in fresh]
+        maps += fresh
     dmap[0] = maps[-1]
+
+    def dcopy(part):
+        return pltpu.make_async_remote_copy(
+            dmap.at[part], drecv.at[part], ds.at[part], dr.at[part],
+            device_id=(tm, y * 2 + (1 - core)), device_id_type=MESH,
+        )
+
+    dcopy(0).start()
     adds = keep * maps[0]
     for h in range(1, hours):
         adds = adds + keep * jnp.exp(-float(h) * srate) * maps[h]
     dmap[1] = adds
-    dcopy = pltpu.make_async_remote_copy(
-        dmap, drecv, ds, dr, device_id=(tm, y * 2 + (1 - core)), device_id_type=MESH
-    )
-    dcopy.start()
+    dcopy(1).start()
     for h in range(hours):
         cum[:, h * factors : (h + 1) * factors] = maps[h]
-    dcopy.wait_recv()
+    dcopy(0).wait_recv()
     mine, other = dmap[0], drecv[0]
     leads = core == 0
     whole = compose(jnp.where(leads, mine, other), jnp.where(leads, other, mine), factors)
     esend[...] = whole
 
-    def ecopy(k):
-        to = lax.rem(g + k, chips)
-        return pltpu.make_async_remote_copy(
-            esend, emaps.at[k], es.at[k], er.at[k],
-            device_id=(pair * 2 + to // ys, lax.rem(to, ys) * 2 + core), device_id_type=MESH,
-        )
-
-    for k in range(1, chips):
-        ecopy(k).start()
+    def slot_peer(slot):
+        return pair * 2 + (a + slot // ys) % 2, lax.rem(y + slot % ys, ys) * 2 + core
+
+    def slot_of(at):
+        return ((a + 2 - at // ys) % 2) * ys + lax.rem(y + ys - at % ys, ys)
+
+    def ecopy(slot):
+        return pltpu.make_async_remote_copy(
+            esend, emaps.at[slot], es.at[slot], er.at[slot],
+            device_id=slot_peer(slot), device_id_type=MESH,
+        )
+
+    bcopy = pltpu.make_async_remote_copy(
+        esend.at[pl.ds(factors, 1)], bin_s, bs, br,
+        device_id=(1, (ys - 1) * 2 + core), device_id_type=MESH,
+    )
+    heads = (pair == 0) & (g == 0)
+
+    @pl.when(heads)
+    def _():
+        bcopy.start()
+
+    slots = [ys] + [slot for slot in range(1, chips) if slot != ys]
+    for slot in slots:
+        ecopy(slot).start()
     emaps[0] = whole
     first = jnp.where(leads, mine, other)
+    dcopy(1).wait_recv()
     mine_adds, other_adds = dmap[1], drecv[1]
     chip_adds = jnp.where(leads, mine_adds, other_adds) + jnp.exp(-float(hours) * srate) * compose(
         first, jnp.where(leads, other_adds, mine_adds), factors
     )
     ssend[...] = chip_adds
 
-    def scopy(k):
-        to = lax.rem(g + k, chips)
-        return pltpu.make_async_remote_copy(
-            ssend, smaps.at[k], ss.at[k], sr.at[k],
-            device_id=(pair * 2 + to // ys, lax.rem(to, ys) * 2 + core), device_id_type=MESH,
-        )
-
-    for k in range(1, chips):
-        scopy(k).start()
+    def scopy(slot):
+        return pltpu.make_async_remote_copy(
+            ssend, smaps.at[slot], ss.at[slot], sr.at[slot],
+            device_id=slot_peer(slot), device_id_type=MESH,
+        )
+
+    for slot in slots:
+        scopy(slot).start()
     smaps[0] = chip_adds
     span = 2 * local
     after = (a + 1) * local
@@ -283,9 +313,39 @@
     tail_w = jnp.where(far >= 0.0, keep[None] * jnp.exp(-jnp.maximum(far, 0.0) * srate[None]), 0.0)
     end_w = jnp.exp(-(span - after).astype(F32) * srate)
     span_w = jnp.exp(-float(span) * srate)
-    for k in range(1, chips):
-        ecopy(k).wait_recv()
-    parts = [emaps[lax.rem(g - at + chips, chips)] for at in range(chips)]
+    def vcopy(far):
+        return pltpu.make_async_remote_copy(
+            vout, vin, vs.at[far - 1], vr,
+            device_id=(lax.rem(tm + 2 * far, tms), ser), device_id_type=MESH,
+        )
+
+    def vstart(to):
+        return pltpu.make_async_remote_copy(
+            vout, vin, vls.at[to], vr,
+            device_id=(2 + to // ys, (to % ys) * 2 + core), device_id_type=MESH,
+        )
+
+    def carry(vector, matrix, shift):
+        column = jnp.sum(jnp.where(eye, vector, 0.0), axis=1, keepdims=True)
+        return jnp.sum(column * matrix, axis=0, keepdims=True) + shift
+
+    for slot in slots[:-1]:
+        ecopy(slot).wait_recv()
+
+    @pl.when(leader)
+    def _():
+        bcopy.wait_recv()
+        state = bin_s[...]
+        for at in range(1, chips):
+            step = emaps[slot_of(at)]
+            state = carry(state, step[:factors], step[factors : factors + 1])
+        vout[...] = state
+        if pairs > 1:
+            for to in range(chips - 1, -1, -1):
+                vstart(to).start()
+
+    ecopy(slots[-1]).wait_recv()
+    parts = [emaps[slot_of(at)] for at in range(chips)]
     level = parts
     while len(level) > 1:
         level = [
@@ -294,12 +354,6 @@
         ]
     total = level[0]
 
-    def vcopy(far):
-        return pltpu.make_async_remote_copy(
-            vout, vin, vs.at[far - 1], vr,
-            device_id=(lax.rem(tm + 2 * far, tms), ser), device_id_type=MESH,
-        )
-
     tcopy = pltpu.make_async_remote_copy(
         tsend, trecv, ts, tr, device_id=(lax.rem(tm + 2, tms), ser), device_id_type=MESH
     )
@@ -314,12 +368,6 @@
     @pl.when(pair == 0)
     def _():
         vcur[...] = jnp.zeros_like(vcur)
-        vout[...] = total[factors : factors + 1]
-        vcopy(1).start()
-
-    def carry(vector, matrix, shift):
-        column = jnp.sum(jnp.where(eye, vector, 0.0), axis=1, keepdims=True)
-        return jnp.sum(column * matrix, axis=0, keepdims=True) + shift
 
     def forward():
         vcopy(1).wait_recv()
@@ -359,10 +407,10 @@
     at_end = pair == pairs - 1
     for k in range(1, chips):
         scopy(k).wait_recv()
-    group_adds = smaps[lax.rem(g, chips)] + jnp.where(at_end, span_w * decays, 0.0) * total
+    group_adds = smaps[slot_of(0)] + jnp.where(at_end, span_w * decays, 0.0) * total
     for at in range(1, chips):
         group_adds = group_adds + jnp.exp(-float(2 * hours * at) * srate) * compose(
-            before_chip[at - 1], smaps[lax.rem(g - at + chips, chips)], factors
+            before_chip[at - 1], smaps[slot_of(at)], factors
         )
     lead_s[:, wide_at:] = halves(group_adds[:factors])
     lead_b = jnp.concatenate([lead_b, group_adds[factors:]], axis=1)
@@ -461,14 +509,26 @@
             copy1(k, h).wait_send()
             if k:
                 copy2(k, h).wait_send()
-    dcopy.wait_send()
+    dcopy(0).wait_send()
+    dcopy(1).wait_send()
     for k in range(1, chips):
         ecopy(k).wait_send()
         scopy(k).wait_send()
 
-    @pl.when((odd | (pair == 0)) & (pair < pairs - 1))
+    @pl.when(odd & (pair < pairs - 1))
     def _():
         vcopy(1).wait_send()
+
+    @pl.when(heads)
+    def _():
+        bcopy.wait_send()
+
+    if pairs > 1:
+
+        @pl.when(leader)
+        def _():
+            for to in range(chips):
+                vstart(to).wait_send()
 
     @pl.when(odd & (pair < pairs - 2))
     def _():
@@ -506,7 +566,7 @@
         rows = factors + 8
         padded = -(-BINS // 8) * 8
         together = 2 if hours % 2 == 0 else 1
-        sets, packed_rows = hours // together, (together + 1) * (factors // 2) + 8
+        sets, packed_rows = hours // together, factors + 8
         vm = pltpu.VMEM
         dma = pltpu.SemaphoreType.DMA
         smoothed, packed = pl.pallas_call(
@@ -545,6 +605,7 @@
                 vm((1, factors), F32),
                 vm((1, factors), F32),
                 vm((1, factors), F32),
+                vm((1, factors), F32),
                 vm((rows, factors), F32),
                 vm((rows, factors), F32),
                 vm((hours, factors), F32),
@@ -559,12 +620,13 @@
                 dma((ys, sets)),
                 dma((ys, sets)),
                 dma((ys, sets)),
-                dma, dma,
+                dma((2,)),
+                dma((2,)),
                 dma((chips,)),
                 dma((chips,)),
                 dma((chips,)),
                 dma((chips,)),
-                dma((2,)), dma, dma, dma,
+                dma((2,)), dma, dma((chips,)), dma, dma, dma, dma,
                 dma((2 * sers,)),
                 dma((2 * sers,)),
                 dma((tms // 2,)),

time: 37.9 us -> 37 us (0.976)
  Pallas kernels: 35.7 us -> 34.8 us
    pallas_call x1, Pallas kernels: 35.7 us -> 34.8 us  [body(): pl.pallas_call(functools.partial(kernel, tms, sers), out_shape=(vm((local...]
where the time goes in v2:
time: 37 us; the launch traced here: 36.9 us
  Pallas kernels  34.8 us (94%)
  local copies, waits for them, and re-layouts  1.36 us (4%)
  between operations  0.64 us (2%)
    pallas_call x1, Pallas kernels, body(): pl.pallas_call(functools.partial(kernel, tms, sers), out_shape=(vm((local...  34.8 us
    unnamed x2, local copies, waits for them, and re-layouts  1.28 us

profile of v2, /device:TPU:0, one launch (start us, length us, event | category | flops | bytes accessed | tf_op | source)
XLA Modules:
  0.0 36.9 jit_solution(11549253767936824013)
XLA Ops:
  0.6 34.8 %shard_map.95 = (f32[16,128]{1,0:T(8,128)S(1)}, f32[3,128]{1,0:T(4,128)S(1)}) custom-call(bf16[16,1024]{1,0:T(8,128)(2,1)} %readings_in.1, s32[16,1024]{1,0:T(8,128)} %present_in.1, bf16[1024,128]{1,0:T(8,128)(2,1)} %loadings_in.1, f32[1,1024]{1,0:T(1,128)} %bitcast.7, f32[1,128]{1,0:T(1,128)} %bitcast.9, f32[1,128]{1,0:T(1,128)} %bitcast.10, ...), custom_call_target="tpu_custom_call" | custom-call | tf_op jit(solution)/shard_map/pallas_call | solution.py:572
  35.5 0.6 %copy.13 = f32[16,128]{1,0:T(8,128)} copy(f32[16,128]{1,0:T(8,128)S(1)} %get-tuple-element.8) | data formatting | bytes 16384
  36.1 0.1 reshape.27
  36.2 0.7 %copy.11 = f32[16,20]{1,0:T(8,128)} copy(f32[16,20]{0,1:T(8,128)S(1)} %fusion) | data formatting | bytes 2560
  (1 shorter events, 0.0 us)

commit v3 on v2

--- a/solution.py
+++ b/solution.py
@@ -35,6 +35,10 @@
     )
     out = jnp.dot(both, right, preferred_element_type=F32)
     return out[: left.shape[0]] + out[left.shape[0] :]
+
+
+def dot_t(left, right):
+    return lax.dot_general(left, right, (((1,), (1,)), ((), ())), preferred_element_type=F32)
 
 
 def dot3(left, right):
@@ -121,14 +125,12 @@
 
     ltf = loadings_ref[...].astype(F32).T
     lt_s[...] = ltf.astype(BF16)
-    sl_s[...] = (ltf * prec_ref[...]).T.astype(BF16)
+    sl_s[...] = (ltf * prec_ref[...]).astype(BF16)
     for item in inputs[2:4]:
         item.wait()
     present = present_ref[...].astype(F32)
     read_f = readings_ref[...].astype(F32)
-    score_s[0:local] = jnp.dot(
-        (read_f * present).astype(BF16), sl_s[...], preferred_element_type=F32
-    )
+    score_s[0:local] = dot_t((read_f * present).astype(BF16), sl_s[...])
     score_s[local:] = jnp.zeros_like(score_s[local:])
 
     together_h = 2 if hours % 2 == 0 else 1
@@ -139,22 +141,20 @@
     upper = lane > sub
     line = lax.broadcasted_iota(jnp.int32, (8, factors), 0)
 
-    def hour_terms(base, dst):
-        lefts = []
-        for j in range(hours):
+    def hour_terms(base, dst, held):
+        rights = []
+        for j in range(len(held) * together_h):
             mask = present_ref[pl.ds(base + j, 1), :].astype(F32)
             mask = jnp.broadcast_to(mask, (16, mask.shape[1])).astype(BF16)
-            left = lt_s[...].reshape(factors // 16, 16, mask.shape[1]) * mask[None]
-            lefts.append(left.reshape(factors, mask.shape[1]))
-        out = jnp.dot(
-            jnp.concatenate(lefts, axis=0), sl_s[...], preferred_element_type=F32
-        )
-        for h in range(sets):
-            at = h * together_h
-            first = out[at * factors : (at + 1) * factors]
+            right = sl_s[...].reshape(factors // 16, 16, mask.shape[1]) * mask[None]
+            rights.append(right.reshape(factors, mask.shape[1]))
+        out = dot_t(lt_s[...], jnp.concatenate(rights, axis=0))
+        for place, h in enumerate(held):
+            at = place * together_h
+            first = out[:, at * factors : (at + 1) * factors]
             tail = jnp.zeros((8, factors), F32)
             if together_h == 2:
-                second = out[(at + 1) * factors : (at + 2) * factors]
+                second = out[:, (at + 1) * factors : (at + 2) * factors]
                 dst[h, :factors] = jnp.where(upper, first, second)
                 corner = jnp.sum(jnp.where(eye, first, 0.0), axis=0, keepdims=True)
                 tail = jnp.where(line == together_h, corner, tail)
@@ -194,17 +194,20 @@
     order = list(range(1, ys)) + [0]
     for place, k in enumerate(order):
         owner = lax.rem(y + k, ys) * 2
-        hour_terms((owner + (1 - core)) * hours, send1.at[k])
-        if place == 0:
-            before = jnp.where(pair > 0, 1, 0) + jnp.where(pair > 1, 1, 0)
-            behind = jnp.where(pair < pairs - 1, 1, 0) + jnp.where(pair < pairs - 2, 1, 0)
-            extra = jnp.where(leader, chips - 1, 0)
-            pl.semaphore_wait(barrier, plane - 1 + before + behind + extra)
-        for h in range(sets):
-            copy1(k, h).start()
-        hour_terms((owner + core) * hours, acc.at[k])
-        if k:
-            for h in range(sets):
+        theirs, ours = (owner + (1 - core)) * hours, (owner + core) * hours
+        groups = [[h] for h in range(sets)] if k else [list(range(sets))]
+        for held in groups:
+            hour_terms(theirs + held[0] * together_h, send1.at[k], held)
+            if place == 0 and held[0] == 0:
+                before = jnp.where(pair > 0, 1, 0) + jnp.where(pair > 1, 1, 0)
+                behind = jnp.where(pair < pairs - 1, 1, 0) + jnp.where(pair < pairs - 2, 1, 0)
+                extra = jnp.where(leader, chips - 1, 0)
+                pl.semaphore_wait(barrier, plane - 1 + before + behind + extra)
+            for h in held:
+                copy1(k, h).start()
+        for held in groups:
+            hour_terms(ours + held[0] * together_h, acc.at[k], held)
+            for h in held if k else []:
                 copy1(k, h).wait_recv()
                 acc[k, h] = acc[k, h] + recv1[k, h]
                 copy2(k, h).start()
@@ -587,7 +590,7 @@
                 vm((1, factors), F32),
                 vm((1, series), regions.dtype),
                 vm((factors, series), BF16),
-                vm((series, factors), BF16),
+                vm((factors, series), BF16),
                 vm((series, 8 * GROUPS), BF16),
                 vm((local + 8, factors), F32),
                 vm((ys, sets, packed_rows, factors), F32),

time: 37 us -> 35.3 us (0.954)
  Pallas kernels: 34.8 us -> 33.2 us
    pallas_call x1, Pallas kernels: 34.8 us -> 33.2 us  [body(): pl.pallas_call(functools.partial(kernel, tms, sers), out_shape=(vm((local...]
where the time goes in v3:
time: 35.3 us; the launch traced here: 35.2 us
  Pallas kernels  33.2 us (94%)
  local copies, waits for them, and re-layouts  1.36 us (4%)
  between operations  0.64 us (2%)
    pallas_call x1, Pallas kernels, body(): pl.pallas_call(functools.partial(kernel, tms, sers), out_shape=(vm((local...  33.2 us
    unnamed x2, local copies, waits for them, and re-layouts  1.28 us

profile of v3, /device:TPU:0, one launch (start us, length us, event | category | flops | bytes accessed | tf_op | source)
XLA Modules:
  0.0 35.2 jit_solution(2016353574192268079)
XLA Ops:
  0.6 33.2 %shard_map.95 = (f32[16,128]{1,0:T(8,128)S(1)}, f32[3,128]{1,0:T(4,128)S(1)}) custom-call(bf16[16,1024]{1,0:T(8,128)(2,1)} %readings_in.1, s32[16,1024]{1,0:T(8,128)} %present_in.1, bf16[1024,128]{1,0:T(8,128)(2,1)} %loadings_in.1, f32[1,1024]{1,0:T(1,128)} %bitcast.7, f32[1,128]{1,0:T(1,128)} %bitcast.9, f32[1,128]{1,0:T(1,128)} %bitcast.10, ...), custom_call_target="tpu_custom_call" | custom-call | tf_op jit(solution)/shard_map/pallas_call | solution.py:575
  33.8 0.6 %copy.13 = f32[16,128]{1,0:T(8,128)} copy(f32[16,128]{1,0:T(8,128)S(1)} %get-tuple-element.8) | data formatting | bytes 16384
  34.4 0.1 reshape.27
  34.5 0.7 %copy.11 = f32[16,20]{1,0:T(8,128)} copy(f32[16,20]{0,1:T(8,128)S(1)} %fusion) | data formatting | bytes 2560
  (1 shorter events, 0.0 us)

commit v4 on v3

--- a/solution.py
+++ b/solution.py
@@ -48,6 +48,30 @@
 def compose(earlier, later, factors):
     out = dot3(earlier, later[:factors])
     return jnp.concatenate([out[:factors], out[factors:] + later[factors:]], axis=0)
+
+
+LINES = -(-BINS // 8)
+
+
+def bin_row(b):
+    return b % LINES * 8 + b // LINES
+
+
+def finish(scale, rows_ref, packed_ref, smoothed_ref, hist_ref, held, sems):
+    rows_out = pltpu.make_async_copy(rows_ref, smoothed_ref, sems.at[0])
+    rows_out.start()
+    packed = packed_ref[...] * scale
+    tall = jnp.concatenate(
+        [packed, jnp.zeros((packed.shape[1] - LINES, packed.shape[1]), F32)], axis=0
+    ).T
+    total = tall[:GROUPS]
+    for j in range(1, 8):
+        total = total + pltpu.roll(tall[j * GROUPS : (j + 1) * GROUPS], LINES * j, 1)
+    held[...] = total[:, :BINS]
+    hist_out = pltpu.make_async_copy(held, hist_ref, sems.at[1])
+    hist_out.start()
+    rows_out.wait()
+    hist_out.wait()
 
 
 def kernel(
@@ -476,12 +500,14 @@
     probab = 0.5 * (1.0 + lax.erf(standard * 0.7071067811865476))
     spot = jnp.where(present_ref[...] > 0, probab * BINS - 0.5, -4.0)
     for b in range(BINS):
-        table[b : b + 1, :] = jnp.sum(
+        at = bin_row(b)
+        table[at : at + 1, :] = jnp.sum(
             jnp.maximum(0.0, 1.0 - jnp.abs(spot - b)), axis=0, keepdims=True
         )
     padded = table.shape[0]
-    if padded > BINS:
-        table[BINS:, :] = jnp.zeros_like(table[BINS:, :])
+    for b in range(BINS, padded):
+        at = bin_row(b)
+        table[at : at + 1, :] = jnp.zeros_like(table[at : at + 1, :])
     th, tl = split2(table[...])
     tally = jnp.dot(
         jnp.concatenate([th, tl], axis=0), mem_s[...], preferred_element_type=F32
@@ -642,8 +668,16 @@
             frate.reshape(1, -1), srate.reshape(1, -1), regions.reshape(1, -1),
         )
         scale = BINS * GROUPS / (local * tms * series * sers)
-        histogram = packed.reshape(-1, GROUPS)[:BINS].T * scale
-        return smoothed, histogram
+        return pl.pallas_call(
+            functools.partial(finish, scale),
+            out_shape=(
+                jax.ShapeDtypeStruct((local, factors), F32),
+                jax.ShapeDtypeStruct((GROUPS, BINS), F32),
+            ),
+            in_specs=[pl.BlockSpec(memory_space=vm)] * 2,
+            out_specs=(pl.BlockSpec(memory_space=pl.ANY),) * 2,
+            scratch_shapes=[vm((GROUPS, BINS), F32), dma((2,))],
+        )(*(pltpu.with_memory_space_constraint(part, vm) for part in (smoothed, packed)))
 
     in_specs = (
         P("tm", "series"), P("tm", "series"), P("series", None), P("series"),

time: 35.3 us -> 34.7 us (0.983)
  local copies, waits for them, and re-layouts: 1.36 us -> 0 us
  Pallas kernels: 33.2 us -> 34 us
    unnamed x2 -> x0, local copies, waits for them, and re-layouts: 1.28 us -> none
    pallas_call x0 -> x1, Pallas kernels: none -> 0.79 us  [body(): pl.pallas_call(functools.partial(finish, scale), out_shape=(jax.ShapeDtyp...]
where the time goes in v4:
time: 34.7 us; the launch traced here: 34.6 us
  Pallas kernels  34 us (98%)
  between operations  0.64 us (2%)
    pallas_call x1, Pallas kernels, body(): pl.pallas_call(functools.partial(kernel, tms, sers), out_shape=(vm((local...  33.2 us
    pallas_call x1, Pallas kernels, body(): pl.pallas_call(functools.partial(finish, scale), out_shape=(jax.ShapeDtyp...  0.79 us

profile of v4, /device:TPU:0, one launch (start us, length us, event | category | flops | bytes accessed | tf_op | source)
XLA Modules:
  0.0 34.6 jit_solution(18389971678427377021)
XLA Ops:
  0.6 33.2 %shard_map.95 = (f32[16,128]{1,0:T(8,128)S(1)}, f32[3,128]{1,0:T(4,128)S(1)}) custom-call(bf16[16,1024]{1,0:T(8,128)(2,1)} %readings_in.1, s32[16,1024]{1,0:T(8,128)} %present_in.1, bf16[1024,128]{1,0:T(8,128)(2,1)} %loadings_in.1, f32[1,1024]{1,0:T(1,128)} %bitcast.5, f32[1,128]{1,0:T(1,128)} %bitcast.7, f32[1,128]{1,0:T(1,128)} %bitcast.8, ...), custom_call_target="tpu_custom_call" | custom-call | tf_op jit(solution)/shard_map/pallas_call | solution.py:601
  33.8 0.8 %shard_map.96 = (f32[16,128]{1,0:T(8,128)}, f32[16,20]{1,0:T(8,128)}) custom-call(f32[16,128]{1,0:T(8,128)S(1)} %get-tuple-element.4.rows_ref, f32[3,128]{1,0:T(4,128)S(1)} %get-tuple-element.5.packed_ref), custom_call_target="tpu_custom_call" | custom-call | tf_op jit(solution)/shard_map/pallas_call | solution.py:671

commit v5 on v4

--- a/solution.py
+++ b/solution.py
@@ -50,23 +50,21 @@
     return jnp.concatenate([out[:factors], out[factors:] + later[factors:]], axis=0)
 
 
-LINES = -(-BINS // 8)
-
-
-def bin_row(b):
-    return b % LINES * 8 + b // LINES
+LINES = -(-(BINS + 2) // 8)
 
 
 def finish(scale, rows_ref, packed_ref, smoothed_ref, hist_ref, held, sems):
     rows_out = pltpu.make_async_copy(rows_ref, smoothed_ref, sems.at[0])
     rows_out.start()
     packed = packed_ref[...] * scale
-    tall = jnp.concatenate(
-        [packed, jnp.zeros((packed.shape[1] - LINES, packed.shape[1]), F32)], axis=0
-    ).T
+    width = packed.shape[1]
+    parts = []
+    for at in range(LINES):
+        parts += [packed[at : at + 1], jnp.zeros((7, width), F32)]
+    tall = jnp.concatenate(parts + [jnp.zeros((width - 8 * LINES, width), F32)], axis=0).T
     total = tall[:GROUPS]
     for j in range(1, 8):
-        total = total + pltpu.roll(tall[j * GROUPS : (j + 1) * GROUPS], LINES * j, 1)
+        total = total + pltpu.roll(tall[j * GROUPS : (j + 1) * GROUPS], j, 1)
     held[...] = total[:, :BINS]
     hist_out = pltpu.make_async_copy(held, hist_ref, sems.at[1])
     hist_out.start()
@@ -79,9 +77,9 @@
     readings_in, present_in, loadings_in, prec_in, gain_in, frate_in, srate_in, regions_in,
     smoothed_ref, hist_ref,
     readings_ref, present_ref, loadings_ref, prec_ref, gain_ref, frate_ref, srate_ref, regions_ref,
-    lt_s, sl_s, mem_s, score_s, send1, recv1, acc, recv2, cum, dmap, drecv, emaps, esend, smaps, ssend, lead_s,
+    lt_s, sl_s, mem_s, score_s, send1, recv1, acc, recv2, cum, dmap, emaps, esend, smaps, ssend, lead_s,
     vin, vout, vcur, bin_s, tsend, trecv, fown, fall, shown, shifts, table, hown, hall,
-    ins, s1s, s1r, s2s, s2r, ds, dr, es, er, ss, sr, vs, vr, vls, bs, br, ts, tr, fs, fr, cs, cr, hs, hr,
+    ins, s1s, s1r, s2s, s2r, ds, dr, es, er, ss, sr, vs, vr, vls, bs, br, ts, tr, there, fs, fr, cs, cr, hs, hr,
 ):
     tm, ser = lax.axis_index("tm"), lax.axis_index("series")
     y, core = ser // 2, ser % 2
@@ -97,6 +95,8 @@
     chips = 2 * ys
     g = a * ys + y
     leader = (pair == 0) & (g == chips - 1)
+    odd = pair % 2 == 1
+    hands_map = (pair % 2 == 0) & (pair > 0) & (pair < pairs - 1)
 
     inputs = [
         pltpu.make_async_copy(src, dst, ins.at[i])
@@ -129,14 +129,6 @@
     @pl.when(pair < pairs - 1)
     def _():
         pl.semaphore_signal(barrier, inc=1, device_id=(tm + 2, ser), device_id_type=MESH)
-
-    @pl.when(pair > 1)
-    def _():
-        pl.semaphore_signal(barrier, inc=1, device_id=(tm - 4, ser), device_id_type=MESH)
-
-    @pl.when(pair < pairs - 2)
-    def _():
-        pl.semaphore_signal(barrier, inc=1, device_id=(tm + 4, ser), device_id_type=MESH)
 
     @pl.when((pair == 1) & (g < chips - 1))
     def _():
@@ -223,10 +215,15 @@
         for held in groups:
             hour_terms(theirs + held[0] * together_h, send1.at[k], held)
             if place == 0 and held[0] == 0:
-                before = jnp.where(pair > 0, 1, 0) + jnp.where(pair > 1, 1, 0)
-                behind = jnp.where(pair < pairs - 1, 1, 0) + jnp.where(pair < pairs - 2, 1, 0)
+                before = jnp.where(pair > 0, 1, 0)
+                behind = jnp.where(pair < pairs - 1, 1, 0)
                 extra = jnp.where(leader, chips - 1, 0)
                 pl.semaphore_wait(barrier, plane - 1 + before + behind + extra)
+
+                @pl.when(hands_map)
+                def _():
+                    pl.semaphore_signal(there, inc=1, device_id=(tm - 2, ser), device_id_type=MESH)
+
             for h in held:
                 copy1(k, h).start()
         for held in groups:
@@ -265,11 +262,11 @@
         if maps:
             fresh = [compose(maps[-1], item, factors) for item in fresh]
         maps += fresh
-    dmap[0] = maps[-1]
+    dmap[core, 0] = maps[-1]
 
     def dcopy(part):
         return pltpu.make_async_remote_copy(
-            dmap.at[part], drecv.at[part], ds.at[part], dr.at[part],
+            dmap.at[core, part], dmap.at[core, part], ds.at[part], dr.at[part],
             device_id=(tm, y * 2 + (1 - core)), device_id_type=MESH,
         )
 
@@ -277,14 +274,14 @@
     adds = keep * maps[0]
     for h in range(1, hours):
         adds = adds + keep * jnp.exp(-float(h) * srate) * maps[h]
-    dmap[1] = adds
+    dmap[core, 1] = adds
     dcopy(1).start()
     for h in range(hours):
         cum[:, h * factors : (h + 1) * factors] = maps[h]
     dcopy(0).wait_recv()
-    mine, other = dmap[0], drecv[0]
     leads = core == 0
-    whole = compose(jnp.where(leads, mine, other), jnp.where(leads, other, mine), factors)
+    first = dmap[0, 0]
+    whole = compose(first, dmap[1, 0], factors)
     esend[...] = whole
 
     def slot_peer(slot):
@@ -313,12 +310,8 @@
     for slot in slots:
         ecopy(slot).start()
     emaps[0] = whole
-    first = jnp.where(leads, mine, other)
     dcopy(1).wait_recv()
-    mine_adds, other_adds = dmap[1], drecv[1]
-    chip_adds = jnp.where(leads, mine_adds, other_adds) + jnp.exp(-float(hours) * srate) * compose(
-        first, jnp.where(leads, other_adds, mine_adds), factors
-    )
+    chip_adds = dmap[0, 1] + jnp.exp(-float(hours) * srate) * compose(first, dmap[1, 1], factors)
     ssend[...] = chip_adds
 
     def scopy(slot):
@@ -384,8 +377,6 @@
     tcopy = pltpu.make_async_remote_copy(
         tsend, trecv, ts, tr, device_id=(lax.rem(tm + 2, tms), ser), device_id_type=MESH
     )
-    odd = pair % 2 == 1
-    hands_map = (pair % 2 == 0) & (pair > 0) & (pair < pairs - 1)
 
     @pl.when(hands_map)
     def _():
@@ -412,6 +403,7 @@
 
             @pl.when(pair < pairs - 2)
             def _():
+                pl.semaphore_wait(there, 1)
                 vcopy(2).start()
 
     @pl.when(pair == 1)
@@ -425,7 +417,7 @@
         start_map = jnp.where(g == at, before_chip[-1], start_map)
         if at + 1 < chips:
             before_chip.append(compose(before_chip[-1], parts[at], factors))
-    start_map = jnp.where(leads, start_map, compose(start_map, other, factors))
+    start_map = jnp.where(leads, start_map, compose(start_map, first, factors))
     cums = cum[...]
     lead = dot3(start_map, cums[:factors])
     wide_at = hours * factors
@@ -499,16 +491,32 @@
     standard = (readings_ref[...].astype(F32) - fitted) * prec_root
     probab = 0.5 * (1.0 + lax.erf(standard * 0.7071067811865476))
     spot = jnp.where(present_ref[...] > 0, probab * BINS - 0.5, -4.0)
-    for b in range(BINS):
-        at = bin_row(b)
-        table[at : at + 1, :] = jnp.sum(
-            jnp.maximum(0.0, 1.0 - jnp.abs(spot - b)), axis=0, keepdims=True
-        )
     padded = table.shape[0]
-    for b in range(BINS, padded):
-        at = bin_row(b)
-        table[at : at + 1, :] = jnp.zeros_like(table[at : at + 1, :])
-    th, tl = split2(table[...])
+    across = lax.broadcasted_iota(jnp.int32, (8, spot.shape[1]), 0)
+    picks = [across % 2 == 0, across // 2 % 2 == 0, across < 4]
+
+    def above(knot):
+        if knot > BINS:
+            return jnp.zeros((8, spot.shape[1]), F32)
+        over = jnp.maximum(0.0, spot - knot)
+        total = over[:8]
+        for at in range(8, local, 8):
+            total = total + over[at : at + 8]
+        return total
+
+    for at in range(0, padded, 8):
+        level = [above(at + i - 1) for i in range(8)]
+        for pick, shift in zip(picks, (1, 2, 4)):
+            level = [
+                jnp.where(pick, x, z) + pltpu.roll(jnp.where(pick, z, x), shift, 0)
+                for x, z in zip(level[::2], level[1::2])
+            ]
+        table[at : at + 8, :] = level[0]
+    sums = table[...]
+    next_sums = pltpu.roll(sums, padded - 1, 0)
+    bins = sums - 2.0 * next_sums + pltpu.roll(sums, padded - 2, 0)
+    bins = jnp.where(lax.broadcasted_iota(jnp.int32, bins.shape, 0) < BINS, bins, 0.0)
+    th, tl = split2(bins)
     tally = jnp.dot(
         jnp.concatenate([th, tl], axis=0), mem_s[...], preferred_element_type=F32
     )
@@ -593,7 +601,7 @@
         n, ys = tms * sers, sers // 2
         chips = 2 * ys
         rows = factors + 8
-        padded = -(-BINS // 8) * 8
+        padded = -(-(BINS + 2) // 8) * 8
         together = 2 if hours % 2 == 0 else 1
         sets, packed_rows = hours // together, factors + 8
         vm = pltpu.VMEM
@@ -624,8 +632,7 @@
                 vm((ys, sets, packed_rows, factors), F32),
                 vm((ys, sets, packed_rows, factors), F32),
                 vm((rows, hours * factors), F32),
-                vm((2, rows, factors), F32),
-                vm((2, rows, factors), F32),
+                vm((2, 2, rows, factors), F32),
                 vm((chips, rows, factors), F32),
                 vm((rows, factors), F32),
                 vm((chips, rows, factors), F32),
@@ -655,7 +662,7 @@
                 dma((chips,)),
                 dma((chips,)),
                 dma((chips,)),
-                dma((2,)), dma, dma((chips,)), dma, dma, dma, dma,
+                dma((2,)), dma, dma((chips,)), dma, dma, dma, dma, pltpu.SemaphoreType.REGULAR,
                 dma((2 * sers,)),
                 dma((2 * sers,)),
                 dma((tms // 2,)),

time: 34.7 us -> 33.6 us (0.968)
  Pallas kernels: 34 us -> 32.8 us
    pallas_call x1, Pallas kernels: 33.2 us -> 32 us  [body(): pl.pallas_call(functools.partial(kernel, tms, sers), out_shape=(vm((local...]
where the time goes in v5:
time: 33.6 us; the launch traced here: 33.4 us
  Pallas kernels  32.8 us (98%)
  between operations  0.64 us (2%)
    pallas_call x1, Pallas kernels, body(): pl.pallas_call(functools.partial(kernel, tms, sers), out_shape=(vm((local...  32 us
    pallas_call x1, Pallas kernels, body(): pl.pallas_call(functools.partial(finish, scale), out_shape=(jax.ShapeDtyp...  0.79 us

profile of v5, /device:TPU:0, one launch (start us, length us, event | category | flops | bytes accessed | tf_op | source)
XLA Modules:
  0.0 33.4 jit_solution(9980334350799409354)
XLA Ops:
  0.6 32.0 %shard_map.95 = (f32[16,128]{1,0:T(8,128)S(1)}, f32[3,128]{1,0:T(4,128)S(1)}) custom-call(bf16[16,1024]{1,0:T(8,128)(2,1)} %readings_in.1, s32[16,1024]{1,0:T(8,128)} %present_in.1, bf16[1024,128]{1,0:T(8,128)(2,1)} %loadings_in.1, f32[1,1024]{1,0:T(1,128)} %bitcast.5, f32[1,128]{1,0:T(1,128)} %bitcast.7, f32[1,128]{1,0:T(1,128)} %bitcast.8, ...), custom_call_target="tpu_custom_call" | custom-call | tf_op jit(solution)/shard_map/pallas_call | solution.py:609
  32.7 0.8 %shard_map.96 = (f32[16,128]{1,0:T(8,128)}, f32[16,20]{1,0:T(8,128)}) custom-call(f32[16,128]{1,0:T(8,128)S(1)} %get-tuple-element.4.rows_ref, f32[3,128]{1,0:T(4,128)S(1)} %get-tuple-element.5.packed_ref), custom_call_target="tpu_custom_call" | custom-call | tf_op jit(solution)/shard_map/pallas_call | solution.py:678

commit v6 on v5

--- a/solution.py
+++ b/solution.py
@@ -21,20 +21,14 @@
 
 def halves(right):
     high, low = split2(right)
-    return jnp.concatenate([high, low], axis=0)
+    return jnp.concatenate([high, low, high], axis=0)
 
 
 def dot_halves(left, right):
     high, low = split2(left)
-    both = jnp.concatenate(
-        [
-            jnp.concatenate([high, high], axis=1),
-            jnp.concatenate([low, jnp.zeros_like(low)], axis=1),
-        ],
-        axis=0,
-    )
-    out = jnp.dot(both, right, preferred_element_type=F32)
-    return out[: left.shape[0]] + out[left.shape[0] :]
+    return jnp.dot(
+        jnp.concatenate([high, high, low], axis=1), right, preferred_element_type=F32
+    )
 
 
 def dot_t(left, right):
@@ -78,8 +72,8 @@
     smoothed_ref, hist_ref,
     readings_ref, present_ref, loadings_ref, prec_ref, gain_ref, frate_ref, srate_ref, regions_ref,
     lt_s, sl_s, mem_s, score_s, send1, recv1, acc, recv2, cum, dmap, emaps, esend, smaps, ssend, lead_s,
-    vin, vout, vcur, bin_s, tsend, trecv, fown, fall, shown, shifts, table, hown, hall,
-    ins, s1s, s1r, s2s, s2r, ds, dr, es, er, ss, sr, vs, vr, vls, bs, br, ts, tr, there, fs, fr, cs, cr, hs, hr,
+    vin, vout, vcur, bin_s, lmaps, tsend, trecv, fown, fall, shown, shifts, table, hown, hall,
+    ins, s1s, s1r, s2s, s2r, ds, dr, es, er, ss, sr, vs, vr, vls, ls, lr, bs, br, ts, tr, there, fs, fr, cs, cr, hs, hr,
 ):
     tm, ser = lax.axis_index("tm"), lax.axis_index("series")
     y, core = ser // 2, ser % 2
@@ -94,7 +88,7 @@
     pairs = tms // 2
     chips = 2 * ys
     g = a * ys + y
-    leader = (pair == 0) & (g == chips - 1)
+    leader = (pair == 0) & (g == chips - 1) & (core == 0)
     odd = pair % 2 == 1
     hands_map = (pair % 2 == 0) & (pair > 0) & (pair < pairs - 1)
 
@@ -130,18 +124,16 @@
     def _():
         pl.semaphore_signal(barrier, inc=1, device_id=(tm + 2, ser), device_id_type=MESH)
 
-    @pl.when((pair == 1) & (g < chips - 1))
-    def _():
-        pl.semaphore_signal(
-            barrier, inc=1, device_id=(1, (ys - 1) * 2 + core), device_id_type=MESH
-        )
+    @pl.when((pair == 1) & ((g < chips - 1) | (core == 1)))
+    def _():
+        pl.semaphore_signal(barrier, inc=1, device_id=(1, (ys - 1) * 2), device_id_type=MESH)
 
     for item in inputs[:2]:
         item.wait()
 
-    ltf = loadings_ref[...].astype(F32).T
-    lt_s[...] = ltf.astype(BF16)
-    sl_s[...] = (ltf * prec_ref[...]).astype(BF16)
+    turned_l = loadings_ref[...].T
+    lt_s[...] = turned_l
+    sl_s[...] = (turned_l.astype(F32) * prec_ref[...]).astype(BF16)
     for item in inputs[2:4]:
         item.wait()
     present = present_ref[...].astype(F32)
@@ -195,15 +187,17 @@
             (matrices[j], jnp.where(line == 0, tail[j : j + 1], 0.0)) for j in range(together_h)
         ]
 
+    used, sent = pl.ds(0, factors + 1), pl.ds(0, factors + together_h + 1)
+
     def copy1(k, h):
         return pltpu.make_async_remote_copy(
-            send1.at[k, h], recv1.at[k, h], s1s.at[k, h], s1r.at[k, h],
+            send1.at[k, h, sent], recv1.at[k, h, sent], s1s.at[k, h], s1r.at[k, h],
             device_id=(tm, y * 2 + (1 - core)), device_id_type=MESH,
         )
 
     def copy2(k, h):
         return pltpu.make_async_remote_copy(
-            acc.at[k, h], recv2.at[k, h], s2s.at[k, h], s2r.at[k, h],
+            acc.at[k, h, sent], recv2.at[k, h, sent], s2s.at[k, h], s2r.at[k, h],
             device_id=(tm, lax.rem(y + k, ys) * 2 + core), device_id_type=MESH,
         )
 
@@ -217,7 +211,7 @@
             if place == 0 and held[0] == 0:
                 before = jnp.where(pair > 0, 1, 0)
                 behind = jnp.where(pair < pairs - 1, 1, 0)
-                extra = jnp.where(leader, chips - 1, 0)
+                extra = jnp.where(leader, 2 * chips - 1, 0)
                 pl.semaphore_wait(barrier, plane - 1 + before + behind + extra)
 
                 @pl.when(hands_map)
@@ -292,15 +286,30 @@
 
     def ecopy(slot):
         return pltpu.make_async_remote_copy(
-            esend, emaps.at[slot], es.at[slot], er.at[slot],
+            esend.at[used], emaps.at[slot, used], es.at[slot], er.at[slot],
             device_id=slot_peer(slot), device_id_type=MESH,
         )
 
     bcopy = pltpu.make_async_remote_copy(
         esend.at[pl.ds(factors, 1)], bin_s, bs, br,
-        device_id=(1, (ys - 1) * 2 + core), device_id_type=MESH,
-    )
-    heads = (pair == 0) & (g == 0)
+        device_id=(1, (ys - 1) * 2), device_id_type=MESH,
+    )
+    heads = (pair == 0) & (g == 0) & (core == 0)
+    half = factors // 2
+
+    def lcopy(of, part):
+        span = pl.ds(0, half) if part == 0 else pl.ds(half, rows - half)
+        return pltpu.make_async_remote_copy(
+            esend.at[span], lmaps.at[of, span], ls.at[part], lr.at[of, part],
+            device_id=(1, (ys - 1) * 2), device_id_type=MESH,
+        )
+
+    helps = (pair == 0) & (g > 0) & (g < chips - 1)
+    for part in range(2):
+
+        @pl.when(helps & (core == part))
+        def _(part=part):
+            lcopy(g, part).start()
 
     @pl.when(heads)
     def _():
@@ -316,7 +325,7 @@
 
     def scopy(slot):
         return pltpu.make_async_remote_copy(
-            ssend, smaps.at[slot], ss.at[slot], sr.at[slot],
+            ssend.at[used], smaps.at[slot, used], ss.at[slot], sr.at[slot],
             device_id=slot_peer(slot), device_id_type=MESH,
         )
 
@@ -342,28 +351,31 @@
     def vstart(to):
         return pltpu.make_async_remote_copy(
             vout, vin, vls.at[to], vr,
-            device_id=(2 + to // ys, (to % ys) * 2 + core), device_id_type=MESH,
-        )
-
-    def carry(vector, matrix, shift):
-        column = jnp.sum(jnp.where(eye, vector, 0.0), axis=1, keepdims=True)
+            device_id=(2 + to // sers, to % sers), device_id_type=MESH,
+        )
+
+    def upright(vector):
+        return jnp.sum(jnp.where(eye, vector, 0.0), axis=1, keepdims=True)
+
+    def carry(column, matrix, shift):
         return jnp.sum(column * matrix, axis=0, keepdims=True) + shift
+
+    @pl.when(leader)
+    def _():
+        bcopy.wait_recv()
+        column = jnp.broadcast_to(upright(bin_s[...]), (factors, factors))
+        for at in range(1, chips - 1):
+            for part in range(2):
+                lcopy(at, part).wait_recv()
+            step = lmaps[at]
+            column = upright(carry(column, step[:factors], step[factors : factors + 1]))
+        vout[...] = carry(column, whole[:factors], whole[factors : factors + 1])
+        if pairs > 1:
+            for to in range(plane - 1, -1, -1):
+                vstart(to).start()
 
     for slot in slots[:-1]:
         ecopy(slot).wait_recv()
-
-    @pl.when(leader)
-    def _():
-        bcopy.wait_recv()
-        state = bin_s[...]
-        for at in range(1, chips):
-            step = emaps[slot_of(at)]
-            state = carry(state, step[:factors], step[factors : factors + 1])
-        vout[...] = state
-        if pairs > 1:
-            for to in range(chips - 1, -1, -1):
-                vstart(to).start()
-
     ecopy(slots[-1]).wait_recv()
     parts = [emaps[slot_of(at)] for at in range(chips)]
     level = parts
@@ -375,7 +387,7 @@
     total = level[0]
 
     tcopy = pltpu.make_async_remote_copy(
-        tsend, trecv, ts, tr, device_id=(lax.rem(tm + 2, tms), ser), device_id_type=MESH
+        tsend.at[used], trecv.at[used], ts, tr, device_id=(lax.rem(tm + 2, tms), ser), device_id_type=MESH
     )
 
     @pl.when(hands_map)
@@ -394,17 +406,18 @@
         @pl.when(odd & (pair > 1))
         def _():
             tcopy.wait_recv()
-            vcur[...] = carry(vin[...], trecv[0:factors], trecv[factors : factors + 1])
+            vcur[...] = carry(upright(vin[...]), trecv[0:factors], trecv[factors : factors + 1])
 
         @pl.when(odd & (pair < pairs - 1))
         def _():
-            vout[...] = carry(vcur[...], total[:factors], total[factors : factors + 1])
-            vcopy(1).start()
+            vout[...] = carry(upright(vcur[...]), total[:factors], total[factors : factors + 1])
 
             @pl.when(pair < pairs - 2)
             def _():
                 pl.semaphore_wait(there, 1)
                 vcopy(2).start()
+
+            vcopy(1).start()
 
     @pl.when(pair == 1)
     def _():
@@ -560,11 +573,17 @@
     def _():
         bcopy.wait_send()
 
+    for part in range(2):
+
+        @pl.when(helps & (core == part))
+        def _(part=part):
+            lcopy(g, part).wait_send()
+
     if pairs > 1:
 
         @pl.when(leader)
         def _():
-            for to in range(chips):
+            for to in range(plane):
                 vstart(to).wait_send()
 
     @pl.when(odd & (pair < pairs - 2))
@@ -637,11 +656,12 @@
                 vm((rows, factors), F32),
                 vm((chips, rows, factors), F32),
                 vm((rows, factors), F32),
-                vm((2 * factors, (hours + 1) * factors), BF16),
+                vm((3 * factors, (hours + 1) * factors), BF16),
                 vm((1, factors), F32),
                 vm((1, factors), F32),
                 vm((1, factors), F32),
                 vm((1, factors), F32),
+                vm((chips, rows, factors), F32),
                 vm((rows, factors), F32),
                 vm((rows, factors), F32),
                 vm((hours, factors), F32),
@@ -662,7 +682,7 @@
                 dma((chips,)),
                 dma((chips,)),
                 dma((chips,)),
-                dma((2,)), dma, dma((chips,)), dma, dma, dma, dma, pltpu.SemaphoreType.REGULAR,
+                dma((2,)), dma, dma((2 * sers,)), dma((2,)), dma((chips, 2)), dma, dma, dma, dma, pltpu.SemaphoreType.REGULAR,
                 dma((2 * sers,)),
                 dma((2 * sers,)),
                 dma((tms // 2,)),

time: 33.6 us -> 32.9 us (0.979)
  Pallas kernels: 32.8 us -> 32.1 us
    pallas_call x1, Pallas kernels: 32 us -> 31.3 us  [body(): pl.pallas_call(functools.partial(kernel, tms, sers), out_shape=(vm((local...]
where the time goes in v6:
time: 32.9 us; the launch traced here: 32.7 us
  Pallas kernels  32.1 us (98%)
  between operations  0.64 us (2%)
    pallas_call x1, Pallas kernels, body(): pl.pallas_call(functools.partial(kernel, tms, sers), out_shape=(vm((local...  31.3 us
    pallas_call x1, Pallas kernels, body(): pl.pallas_call(functools.partial(finish, scale), out_shape=(jax.ShapeDtyp...  0.79 us

profile of v6, /device:TPU:0, one launch (start us, length us, event | category | flops | bytes accessed | tf_op | source)
XLA Modules:
  0.0 32.7 jit_solution(6800034265755520595)
XLA Ops:
  0.6 31.3 %shard_map.95 = (f32[16,128]{1,0:T(8,128)S(1)}, f32[3,128]{1,0:T(4,128)S(1)}) custom-call(bf16[16,1024]{1,0:T(8,128)(2,1)} %readings_in.1, s32[16,1024]{1,0:T(8,128)} %present_in.1, bf16[1024,128]{1,0:T(8,128)(2,1)} %loadings_in.1, f32[1,1024]{1,0:T(1,128)} %bitcast.5, f32[1,128]{1,0:T(1,128)} %bitcast.7, f32[1,128]{1,0:T(1,128)} %bitcast.8, ...), custom_call_target="tpu_custom_call" | custom-call | tf_op jit(solution)/shard_map/pallas_call | solution.py:628
  32.0 0.8 %shard_map.96 = (f32[16,128]{1,0:T(8,128)}, f32[16,20]{1,0:T(8,128)}) custom-call(f32[16,128]{1,0:T(8,128)S(1)} %get-tuple-element.4.rows_ref, f32[3,128]{1,0:T(4,128)S(1)} %get-tuple-element.5.packed_ref), custom_call_target="tpu_custom_call" | custom-call | tf_op jit(solution)/shard_map/pallas_call | solution.py:698

commit v7 on v6

--- a/solution.py
+++ b/solution.py
@@ -71,8 +71,8 @@
     readings_in, present_in, loadings_in, prec_in, gain_in, frate_in, srate_in, regions_in,
     smoothed_ref, hist_ref,
     readings_ref, present_ref, loadings_ref, prec_ref, gain_ref, frate_ref, srate_ref, regions_ref,
-    lt_s, sl_s, mem_s, score_s, send1, recv1, acc, recv2, cum, dmap, emaps, esend, smaps, ssend, lead_s,
-    vin, vout, vcur, bin_s, lmaps, tsend, trecv, fown, fall, shown, shifts, table, hown, hall,
+    lt_s, sl_s, mem_s, send1, recv1, acc, recv2, cum, dmap, emaps, esend, smaps, ssend, lead_s,
+    vin, vout, vcur, bin_s, lmaps, tsend, trecv, fown, fall, shown, shifts, group_s, table, hown, hall,
     ins, s1s, s1r, s2s, s2r, ds, dr, es, er, ss, sr, vs, vr, vls, ls, lr, bs, br, ts, tr, there, fs, fr, cs, cr, hs, hr,
 ):
     tm, ser = lax.axis_index("tm"), lax.axis_index("series")
@@ -132,14 +132,11 @@
         item.wait()
 
     turned_l = loadings_ref[...].T
-    lt_s[...] = turned_l
+    lt_s[:factors] = turned_l
     sl_s[...] = (turned_l.astype(F32) * prec_ref[...]).astype(BF16)
     for item in inputs[2:4]:
         item.wait()
-    present = present_ref[...].astype(F32)
-    read_f = readings_ref[...].astype(F32)
-    score_s[0:local] = dot_t((read_f * present).astype(BF16), sl_s[...])
-    score_s[local:] = jnp.zeros_like(score_s[local:])
+    lt_s[factors:] = readings_ref[...].astype(BF16)
 
     together_h = 2 if hours % 2 == 0 else 1
     sets = hours // together_h
@@ -148,6 +145,7 @@
     eye = sub == lane
     upper = lane > sub
     line = lax.broadcasted_iota(jnp.int32, (8, factors), 0)
+    which = lax.broadcasted_iota(jnp.int32, (local, factors), 0)
 
     def hour_terms(base, dst, held):
         rights = []
@@ -159,17 +157,18 @@
         out = dot_t(lt_s[...], jnp.concatenate(rights, axis=0))
         for place, h in enumerate(held):
             at = place * together_h
-            first = out[:, at * factors : (at + 1) * factors]
+            first = out[:factors, at * factors : (at + 1) * factors]
             tail = jnp.zeros((8, factors), F32)
             if together_h == 2:
-                second = out[:, (at + 1) * factors : (at + 2) * factors]
+                second = out[:factors, (at + 1) * factors : (at + 2) * factors]
                 dst[h, :factors] = jnp.where(upper, first, second)
                 corner = jnp.sum(jnp.where(eye, first, 0.0), axis=0, keepdims=True)
                 tail = jnp.where(line == together_h, corner, tail)
             else:
                 dst[h, :factors] = first
             for j in range(together_h):
-                row = jnp.broadcast_to(score_s[pl.ds(base + at + j, 1), :], (8, factors))
+                row = out[factors:, (at + j) * factors : (at + j + 1) * factors]
+                row = jnp.sum(jnp.where(which == base + at + j, row, 0.0), axis=0, keepdims=True)
                 tail = jnp.where(line == j, row, tail)
             dst[h, factors:] = tail
 
@@ -323,14 +322,22 @@
     chip_adds = dmap[0, 1] + jnp.exp(-float(hours) * srate) * compose(first, dmap[1, 1], factors)
     ssend[...] = chip_adds
 
-    def scopy(slot):
-        return pltpu.make_async_remote_copy(
-            ssend.at[used], smaps.at[slot, used], ss.at[slot], sr.at[slot],
-            device_id=slot_peer(slot), device_id_type=MESH,
-        )
-
-    for slot in slots:
-        scopy(slot).start()
+    def scopy(slot, part):
+        span = pl.ds(0, half) if part == 0 else pl.ds(half, half + 1)
+        row, column = slot_peer(slot)
+        return pltpu.make_async_remote_copy(
+            ssend.at[span], smaps.at[slot, span], ss.at[slot], sr.at[slot, part],
+            device_id=(row, column - core), device_id_type=MESH,
+        )
+
+    sums = (core == 0) & (pair > 0)
+    for part in range(2):
+
+        @pl.when((pair > 0) & (core == part))
+        def _(part=part):
+            for slot in slots:
+                scopy(slot, part).start()
+
     smaps[0] = chip_adds
     span = 2 * local
     after = (a + 1) * local
@@ -433,41 +440,48 @@
     start_map = jnp.where(leads, start_map, compose(start_map, first, factors))
     cums = cum[...]
     lead = dot3(start_map, cums[:factors])
-    wide_at = hours * factors
-    lead_s[:, :wide_at] = halves(lead[:factors])
+    lead_s[...] = halves(lead[:factors])
     lead_b = lead[factors:] + cums[factors:]
     at_end = pair == pairs - 1
-    for k in range(1, chips):
-        scopy(k).wait_recv()
-    group_adds = smaps[slot_of(0)] + jnp.where(at_end, span_w * decays, 0.0) * total
-    for at in range(1, chips):
-        group_adds = group_adds + jnp.exp(-float(2 * hours * at) * srate) * compose(
-            before_chip[at - 1], smaps[slot_of(at)], factors
-        )
-    lead_s[:, wide_at:] = halves(group_adds[:factors])
-    lead_b = jnp.concatenate([lead_b, group_adds[factors:]], axis=1)
+
+    @pl.when(sums)
+    def _():
+        for slot in range(1, chips):
+            for part in range(2):
+                scopy(slot, part).wait_recv()
+        group_adds = smaps[slot_of(0)] + jnp.where(at_end, span_w * decays, 0.0) * total
+        for at in range(1, chips):
+            group_adds = group_adds + jnp.exp(-float(2 * hours * at) * srate) * compose(
+                before_chip[at - 1], smaps[slot_of(at)], factors
+            )
+        group_s[...] = group_adds
 
     @pl.when(pair > 1)
     def _():
         forward()
+
+    def ccopy(to, of, side):
+        return pltpu.make_async_remote_copy(
+            shown, shifts.at[of], cs.at[to, side], cr.at[of],
+            device_id=(to * 2 + a, y * 2 + side), device_id_type=MESH,
+        )
+
+    @pl.when(sums)
+    def _():
+        shown[...] = carry(
+            upright(vcur[...]), group_s[0:factors], group_s[factors : factors + 1]
+        )
+
+        @pl.loop(0, pair)
+        def _(to):
+            for side in range(2):
+                ccopy(to, pair, side).start()
 
     current = jnp.broadcast_to(vcur[...], (8, factors))
     filtered = dot_halves(current, lead_s[...]) + lead_b
     for h in range(hours):
         row = filtered[0:1, h * factors : (h + 1) * factors]
         fown[h : h + 1, :] = row
-    shown[...] = filtered[:, hours * factors :]
-
-    def ccopy(to, of):
-        return pltpu.make_async_remote_copy(
-            shown, shifts.at[of], cs.at[to], cr.at[of],
-            device_id=(to * 2 + a, ser), device_id_type=MESH,
-        )
-
-    @pl.loop(0, pair)
-    def _(to):
-        ccopy(to, pair).start()
-
     fall[place_in] = fown[...]
 
     def fcopy(k):
@@ -483,24 +497,28 @@
         fcopy(k).wait_recv()
     together = fall[...]
     ending = decays * together[plane - 1][hours - 1 : hours]
-    follow = jnp.sum(jnp.sum(together * tail_w, axis=0), axis=0, keepdims=True)
+    tail = jnp.sum(jnp.sum(together * tail_w, axis=0), axis=0, keepdims=True)
+    rows_in = keep * jnp.concatenate([fall[a * sers + s] for s in range(sers)], axis=0)
+    row_at = lax.broadcasted_iota(jnp.int32, (local, factors), 0)
+    reach = 1
+    while reach < local:
+        later = jnp.where(row_at < local - reach, pltpu.roll(rows_in, local - reach, 0), 0.0)
+        rows_in = rows_in + jnp.exp(-float(reach) * srate) * later
+        reach *= 2
+    fade = jnp.exp(-(local - row_at).astype(F32) * srate)
+    rows_in = rows_in + fade * tail
 
     def gather(of, held):
         total, weight = held
-        ccopy(pair, of).wait_recv()
-        return total + weight * shifts[of][0:1], weight * span_w
+        ccopy(pair, of, 0).wait_recv()
+        return total + weight * shifts[of], weight * span_w
 
     beyond, _ = lax.fori_loop(
         pair + 1, pairs, gather, (jnp.where(at_end, ending, 0.0), jnp.ones_like(span_w))
     )
-    follow = follow + end_w * beyond
-    for s in range(sers - 1, -1, -1):
-        block = fall[a * sers + s]
-        for h in range(hours - 1, -1, -1):
-            follow = keep * block[h : h + 1] + retain * follow
-            smoothed_ref[s * hours + h : s * hours + h + 1, :] = follow
-
-    fitted = jnp.dot(smoothed_ref[...].astype(BF16), lt_s[...], preferred_element_type=F32)
+    smoothed_rows = rows_in + fade * (end_w * beyond)
+    smoothed_ref[...] = smoothed_rows
+    fitted = jnp.dot(smoothed_rows.astype(BF16), lt_s[:factors], preferred_element_type=F32)
     standard = (readings_ref[...].astype(F32) - fitted) * prec_root
     probab = 0.5 * (1.0 + lax.erf(standard * 0.7071067811865476))
     spot = jnp.where(present_ref[...] > 0, probab * BINS - 0.5, -4.0)
@@ -525,9 +543,9 @@
                 for x, z in zip(level[::2], level[1::2])
             ]
         table[at : at + 8, :] = level[0]
-    sums = table[...]
-    next_sums = pltpu.roll(sums, padded - 1, 0)
-    bins = sums - 2.0 * next_sums + pltpu.roll(sums, padded - 2, 0)
+    knots = table[...]
+    next_knots = pltpu.roll(knots, padded - 1, 0)
+    bins = knots - 2.0 * next_knots + pltpu.roll(knots, padded - 2, 0)
     bins = jnp.where(lax.broadcasted_iota(jnp.int32, bins.shape, 0) < BINS, bins, 0.0)
     th, tl = split2(bins)
     tally = jnp.dot(
@@ -542,7 +560,9 @@
 
     def hsend(k):
         at = lax.rem(place_in + (plane - 1 - k % plane), plane)
-        to = lax.rem(pair + (pairs - 1 - k // plane), pairs)
+        turn = k // plane
+        step = jnp.where(pair * 2 < pairs, pairs - 1 - turn, lax.rem(turn + 1, pairs))
+        to = lax.rem(pair + step, pairs)
         pltpu.make_async_remote_copy(
             hown, hall.at[me], hs, hr,
             device_id=(to * 2 + at // sers, lax.rem(at, sers)), device_id_type=MESH,
@@ -563,11 +583,17 @@
     dcopy(1).wait_send()
     for k in range(1, chips):
         ecopy(k).wait_send()
-        scopy(k).wait_send()
 
     @pl.when(odd & (pair < pairs - 1))
     def _():
         vcopy(1).wait_send()
+
+    for part in range(2):
+
+        @pl.when((pair > 0) & (core == part))
+        def _(part=part):
+            for slot in slots:
+                scopy(slot, part).wait_send()
 
     @pl.when(heads)
     def _():
@@ -597,9 +623,12 @@
     for k in range(1, plane):
         fcopy(k).wait_send()
 
-    @pl.loop(0, pair)
-    def _(to):
-        ccopy(to, pair).wait_send()
+    @pl.when(sums)
+    def _():
+        @pl.loop(0, pair)
+        def _(to):
+            for side in range(2):
+                ccopy(to, pair, side).wait_send()
 
     hdrain = pltpu.make_async_remote_copy(
         hall.at[pl.ds(0, n - 1)], hall.at[pl.ds(0, n - 1)], hs, hr,
@@ -642,10 +671,9 @@
                 vm((1, factors), F32),
                 vm((1, factors), F32),
                 vm((1, series), regions.dtype),
-                vm((factors, series), BF16),
+                vm((factors + local, series), BF16),
                 vm((factors, series), BF16),
                 vm((series, 8 * GROUPS), BF16),
-                vm((local + 8, factors), F32),
                 vm((ys, sets, packed_rows, factors), F32),
                 vm((ys, sets, packed_rows, factors), F32),
                 vm((ys, sets, packed_rows, factors), F32),
@@ -656,7 +684,7 @@
                 vm((rows, factors), F32),
                 vm((chips, rows, factors), F32),
                 vm((rows, factors), F32),
-                vm((3 * factors, (hours + 1) * factors), BF16),
+                vm((3 * factors, hours * factors), BF16),
                 vm((1, factors), F32),
                 vm((1, factors), F32),
                 vm((1, factors), F32),
@@ -666,8 +694,9 @@
                 vm((rows, factors), F32),
                 vm((hours, factors), F32),
                 vm((2 * sers, hours, factors), F32),
-                vm((8, factors), F32),
-                vm((tms // 2, 8, factors), F32),
+                vm((1, factors), F32),
+                vm((tms // 2, 1, factors), F32),
+                vm((rows, factors), F32),
                 vm((padded, series), F32),
                 vm((padded // 8, 8 * GROUPS), F32),
                 vm((n, padded // 8, 8 * GROUPS), F32),
@@ -681,11 +710,11 @@
                 dma((chips,)),
                 dma((chips,)),
                 dma((chips,)),
-                dma((chips,)),
+                dma((chips, 2)),
                 dma((2,)), dma, dma((2 * sers,)), dma((2,)), dma((chips, 2)), dma, dma, dma, dma, pltpu.SemaphoreType.REGULAR,
                 dma((2 * sers,)),
                 dma((2 * sers,)),
-                dma((tms // 2,)),
+                dma((tms // 2, 2)),
                 dma((tms // 2,)),
                 dma, dma,
             ],

time: 32.9 us -> 32.7 us (level)
  no operation moved by 1% of the time
where the time goes in v7:
time: 32.7 us; the launch traced here: 32.6 us
  Pallas kernels  31.9 us (98%)
  between operations  0.64 us (2%)
    pallas_call x1, Pallas kernels, body(): pl.pallas_call(functools.partial(kernel, tms, sers), out_shape=(vm((local...  31.1 us
    pallas_call x1, Pallas kernels, body(): pl.pallas_call(functools.partial(finish, scale), out_shape=(jax.ShapeDtyp...  0.79 us

profile of v7, /device:TPU:0, one launch (start us, length us, event | category | flops | bytes accessed | tf_op | source)
XLA Modules:
  0.0 32.6 jit_solution(12163139449397570892)
XLA Ops:
  0.6 31.1 %shard_map.95 = (f32[16,128]{1,0:T(8,128)S(1)}, f32[3,128]{1,0:T(4,128)S(1)}) custom-call(bf16[16,1024]{1,0:T(8,128)(2,1)} %readings_in.1, s32[16,1024]{1,0:T(8,128)} %present_in.1, bf16[1024,128]{1,0:T(8,128)(2,1)} %loadings_in.1, f32[1,1024]{1,0:T(1,128)} %bitcast.5, f32[1,128]{1,0:T(1,128)} %bitcast.7, f32[1,128]{1,0:T(1,128)} %bitcast.8, ...), custom_call_target="tpu_custom_call" | custom-call | tf_op jit(solution)/shard_map/pallas_call | solution.py:657
  31.8 0.8 %shard_map.96 = (f32[16,128]{1,0:T(8,128)}, f32[16,20]{1,0:T(8,128)}) custom-call(f32[16,128]{1,0:T(8,128)S(1)} %get-tuple-element.4.rows_ref, f32[3,128]{1,0:T(4,128)S(1)} %get-tuple-element.5.packed_ref), custom_call_target="tpu_custom_call" | custom-call | tf_op jit(solution)/shard_map/pallas_call | solution.py:727

commit v8 on v7

--- a/solution.py
+++ b/solution.py
@@ -120,6 +120,10 @@
     def _():
         pl.semaphore_signal(barrier, inc=1, device_id=(tm - 2, ser), device_id_type=MESH)
 
+    @pl.when((pair > 0) & (core == 1))
+    def _():
+        pl.semaphore_signal(barrier, inc=1, device_id=(tm - 2, y * 2), device_id_type=MESH)
+
     @pl.when(pair < pairs - 1)
     def _():
         pl.semaphore_signal(barrier, inc=1, device_id=(tm + 2, ser), device_id_type=MESH)
@@ -209,13 +213,13 @@
             hour_terms(theirs + held[0] * together_h, send1.at[k], held)
             if place == 0 and held[0] == 0:
                 before = jnp.where(pair > 0, 1, 0)
-                behind = jnp.where(pair < pairs - 1, 1, 0)
+                behind = jnp.where(pair < pairs - 1, 2 - core, 0)
                 extra = jnp.where(leader, 2 * chips - 1, 0)
                 pl.semaphore_wait(barrier, plane - 1 + before + behind + extra)
 
-                @pl.when(hands_map)
+                @pl.when(hands_map & (core == 0))
                 def _():
-                    pl.semaphore_signal(there, inc=1, device_id=(tm - 2, ser), device_id_type=MESH)
+                    pl.semaphore_signal(there, inc=1, device_id=(tm - 2, y * 2), device_id_type=MESH)
 
             for h in held:
                 copy1(k, h).start()
@@ -283,10 +287,15 @@
     def slot_of(at):
         return ((a + 2 - at // ys) % 2) * ys + lax.rem(y + ys - at % ys, ys)
 
-    def ecopy(slot):
-        return pltpu.make_async_remote_copy(
-            esend.at[used], emaps.at[slot, used], es.at[slot], er.at[slot],
-            device_id=slot_peer(slot), device_id_type=MESH,
+    half = factors // 2
+    spans = [pl.ds(0, half), pl.ds(half, half + 1)]
+
+    def ecopy(slot, side, part):
+        row, column = slot_peer(slot)
+        return pltpu.make_async_remote_copy(
+            esend.at[spans[part]], emaps.at[slot, spans[part]],
+            es.at[slot, side], er.at[slot, part],
+            device_id=(row, column - core + side), device_id_type=MESH,
         )
 
     bcopy = pltpu.make_async_remote_copy(
@@ -294,7 +303,6 @@
         device_id=(1, (ys - 1) * 2), device_id_type=MESH,
     )
     heads = (pair == 0) & (g == 0) & (core == 0)
-    half = factors // 2
 
     def lcopy(of, part):
         span = pl.ds(0, half) if part == 0 else pl.ds(half, rows - half)
@@ -315,8 +323,20 @@
         bcopy.start()
 
     slots = [ys] + [slot for slot in range(1, chips) if slot != ys]
-    for slot in slots:
-        ecopy(slot).start()
+    for part in range(2):
+
+        @pl.when((core == part) & (pair > 0))
+        def _(part=part):
+            for side in range(2):
+                for slot in slots:
+                    ecopy(slot, side, part).start()
+
+        @pl.when((core == part) & (pair == 0))
+        def _(part=part):
+            for slot in slots:
+                for side in range(2):
+                    ecopy(slot, side, part).start()
+
     emaps[0] = whole
     dcopy(1).wait_recv()
     chip_adds = dmap[0, 1] + jnp.exp(-float(hours) * srate) * compose(first, dmap[1, 1], factors)
@@ -349,10 +369,10 @@
     tail_w = jnp.where(far >= 0.0, keep[None] * jnp.exp(-jnp.maximum(far, 0.0) * srate[None]), 0.0)
     end_w = jnp.exp(-(span - after).astype(F32) * srate)
     span_w = jnp.exp(-float(span) * srate)
-    def vcopy(far):
-        return pltpu.make_async_remote_copy(
-            vout, vin, vs.at[far - 1], vr,
-            device_id=(lax.rem(tm + 2 * far, tms), ser), device_id_type=MESH,
+    def vcopy(far, side):
+        return pltpu.make_async_remote_copy(
+            vout, vin, vs.at[far - 1, side], vr,
+            device_id=(lax.rem(tm + 2 * far, tms), y * 2 + side), device_id_type=MESH,
         )
 
     def vstart(to):
@@ -378,12 +398,14 @@
             column = upright(carry(column, step[:factors], step[factors : factors + 1]))
         vout[...] = carry(column, whole[:factors], whole[factors : factors + 1])
         if pairs > 1:
-            for to in range(plane - 1, -1, -1):
+            for to in range(plane):
                 vstart(to).start()
 
     for slot in slots[:-1]:
-        ecopy(slot).wait_recv()
-    ecopy(slots[-1]).wait_recv()
+        for part in range(2):
+            ecopy(slot, 0, part).wait_recv()
+    for part in range(2):
+        ecopy(slots[-1], 0, part).wait_recv()
     parts = [emaps[slot_of(at)] for at in range(chips)]
     level = parts
     while len(level) > 1:
@@ -393,38 +415,43 @@
         ]
     total = level[0]
 
-    tcopy = pltpu.make_async_remote_copy(
-        tsend.at[used], trecv.at[used], ts, tr, device_id=(lax.rem(tm + 2, tms), ser), device_id_type=MESH
-    )
-
-    @pl.when(hands_map)
+    def tcopy(side):
+        return pltpu.make_async_remote_copy(
+            tsend.at[used], trecv.at[used], ts.at[side], tr,
+            device_id=(lax.rem(tm + 2, tms), y * 2 + side), device_id_type=MESH,
+        )
+
+    @pl.when(hands_map & (core == 0))
     def _():
         tsend[...] = total
-        tcopy.start()
+        for side in range(2):
+            tcopy(side).start()
 
     @pl.when(pair == 0)
     def _():
         vcur[...] = jnp.zeros_like(vcur)
 
     def forward():
-        vcopy(1).wait_recv()
+        vcopy(1, 0).wait_recv()
         vcur[...] = vin[...]
 
         @pl.when(odd & (pair > 1))
         def _():
-            tcopy.wait_recv()
+            tcopy(0).wait_recv()
             vcur[...] = carry(upright(vin[...]), trecv[0:factors], trecv[factors : factors + 1])
 
-        @pl.when(odd & (pair < pairs - 1))
+        @pl.when(odd & (pair < pairs - 1) & (core == 0))
         def _():
             vout[...] = carry(upright(vcur[...]), total[:factors], total[factors : factors + 1])
 
             @pl.when(pair < pairs - 2)
             def _():
                 pl.semaphore_wait(there, 1)
-                vcopy(2).start()
-
-            vcopy(1).start()
+                for side in range(2):
+                    vcopy(2, side).start()
+
+            for side in range(2):
+                vcopy(1, side).start()
 
     @pl.when(pair == 1)
     def _():
@@ -581,12 +608,19 @@
                 copy2(k, h).wait_send()
     dcopy(0).wait_send()
     dcopy(1).wait_send()
-    for k in range(1, chips):
-        ecopy(k).wait_send()
-
-    @pl.when(odd & (pair < pairs - 1))
-    def _():
-        vcopy(1).wait_send()
+    for part in range(2):
+
+        @pl.when(core == part)
+        def _(part=part):
+            for side in range(2):
+                for slot in slots:
+                    ecopy(slot, side, part).wait_send()
+
+
+    @pl.when(odd & (pair < pairs - 1) & (core == 0))
+    def _():
+        for side in range(2):
+            vcopy(1, side).wait_send()
 
     for part in range(2):
 
@@ -612,13 +646,15 @@
             for to in range(plane):
                 vstart(to).wait_send()
 
-    @pl.when(odd & (pair < pairs - 2))
-    def _():
-        vcopy(2).wait_send()
-
-    @pl.when(hands_map)
-    def _():
-        tcopy.wait_send()
+    @pl.when(odd & (pair < pairs - 2) & (core == 0))
+    def _():
+        for side in range(2):
+            vcopy(2, side).wait_send()
+
+    @pl.when(hands_map & (core == 0))
+    def _():
+        for side in range(2):
+            tcopy(side).wait_send()
 
     for k in range(1, plane):
         fcopy(k).wait_send()
@@ -707,11 +743,11 @@
                 dma((ys, sets)),
                 dma((2,)),
                 dma((2,)),
-                dma((chips,)),
-                dma((chips,)),
+                dma((chips, 2)),
+                dma((chips, 2)),
                 dma((chips,)),
                 dma((chips, 2)),
-                dma((2,)), dma, dma((2 * sers,)), dma((2,)), dma((chips, 2)), dma, dma, dma, dma, pltpu.SemaphoreType.REGULAR,
+                dma((2, 2)), dma, dma((2 * sers,)), dma((2,)), dma((chips, 2)), dma, dma, dma((2,)), dma, pltpu.SemaphoreType.REGULAR,
                 dma((2 * sers,)),
                 dma((2 * sers,)),
                 dma((tms // 2, 2)),

time: 32.7 us -> 32.6 us (level)
  no operation moved by 1% of the time
where the time goes in v8:
time: 32.6 us; the launch traced here: 32.5 us
  Pallas kernels  31.8 us (98%)
  between operations  0.64 us (2%)
    pallas_call x1, Pallas kernels, body(): pl.pallas_call(functools.partial(kernel, tms, sers), out_shape=(vm((local...  31 us
    pallas_call x1, Pallas kernels, body(): pl.pallas_call(functools.partial(finish, scale), out_shape=(jax.ShapeDtyp...  0.79 us

profile of v8, /device:TPU:0, one launch (start us, length us, event | category | flops | bytes accessed | tf_op | source)
XLA Modules:
  0.0 32.5 jit_solution(15031463447162296563)
XLA Ops:
  0.6 31.0 %shard_map.95 = (f32[16,128]{1,0:T(8,128)S(1)}, f32[3,128]{1,0:T(4,128)S(1)}) custom-call(bf16[16,1024]{1,0:T(8,128)(2,1)} %readings_in.1, s32[16,1024]{1,0:T(8,128)} %present_in.1, bf16[1024,128]{1,0:T(8,128)(2,1)} %loadings_in.1, f32[1,1024]{1,0:T(1,128)} %bitcast.5, f32[1,128]{1,0:T(1,128)} %bitcast.7, f32[1,128]{1,0:T(1,128)} %bitcast.8, ...), custom_call_target="tpu_custom_call" | custom-call | tf_op jit(solution)/shard_map/pallas_call | solution.py:693
  31.7 0.8 %shard_map.96 = (f32[16,128]{1,0:T(8,128)}, f32[16,20]{1,0:T(8,128)}) custom-call(f32[16,128]{1,0:T(8,128)S(1)} %get-tuple-element.4.rows_ref, f32[3,128]{1,0:T(4,128)S(1)} %get-tuple-element.5.packed_ref), custom_call_target="tpu_custom_call" | custom-call | tf_op jit(solution)/shard_map/pallas_call | solution.py:763

commit v9 on v8

--- a/solution.py
+++ b/solution.py
@@ -55,7 +55,8 @@
     parts = []
     for at in range(LINES):
         parts += [packed[at : at + 1], jnp.zeros((7, width), F32)]
-    tall = jnp.concatenate(parts + [jnp.zeros((width - 8 * LINES, width), F32)], axis=0).T
+    tall = jnp.concatenate(parts, axis=0).T
+    tall = jnp.concatenate([tall, jnp.zeros((width, width - 8 * LINES), F32)], axis=1)
     total = tall[:GROUPS]
     for j in range(1, 8):
         total = total + pltpu.roll(tall[j * GROUPS : (j + 1) * GROUPS], j, 1)

time: 32.6 us -> 32.6 us (level)
  no operation moved by 1% of the time
where the time goes in v9:
time: 32.6 us; the launch traced here: 32.5 us
  Pallas kernels  31.8 us (98%)
  between operations  0.64 us (2%)
    pallas_call x1, Pallas kernels, body(): pl.pallas_call(functools.partial(kernel, tms, sers), out_shape=(vm((local...  31 us
    pallas_call x1, Pallas kernels, body(): pl.pallas_call(functools.partial(finish, scale), out_shape=(jax.ShapeDtyp...  0.79 us

profile of v9, /device:TPU:0, one launch (start us, length us, event | category | flops | bytes accessed | tf_op | source)
XLA Modules:
  0.0 32.5 jit_solution(3846495251953814803)
XLA Ops:
  0.6 31.0 %shard_map.95 = (f32[16,128]{1,0:T(8,128)S(1)}, f32[3,128]{1,0:T(4,128)S(1)}) custom-call(bf16[16,1024]{1,0:T(8,128)(2,1)} %readings_in.1, s32[16,1024]{1,0:T(8,128)} %present_in.1, bf16[1024,128]{1,0:T(8,128)(2,1)} %loadings_in.1, f32[1,1024]{1,0:T(1,128)} %bitcast.5, f32[1,128]{1,0:T(1,128)} %bitcast.7, f32[1,128]{1,0:T(1,128)} %bitcast.8, ...), custom_call_target="tpu_custom_call" | custom-call | tf_op jit(solution)/shard_map/pallas_call | solution.py:694
  31.7 0.8 %shard_map.96 = (f32[16,128]{1,0:T(8,128)}, f32[16,20]{1,0:T(8,128)}) custom-call(f32[16,128]{1,0:T(8,128)S(1)} %get-tuple-element.4.rows_ref, f32[3,128]{1,0:T(4,128)S(1)} %get-tuple-element.5.packed_ref), custom_call_target="tpu_custom_call" | custom-call | tf_op jit(solution)/shard_map/pallas_call | solution.py:764
